TPU v7x, 32 devices: a whole 2x2x4 slice. The times are simulated.
32 devices in a mesh: inner: 2 (over core), outer: 16 (over z, y, x).
Axes of the slice: x: 2, y: 2, z: 4, core: 2. Of those that a mesh axis runs over, the one named last changes fastest.
Arguments:
- images: bfloat16 [32, 4, 256, 1152], P(('inner', 'outer')), may hold values from -6 to 6
- counts: int32 [32], P(('inner', 'outer')), may hold values from 1 to 4, as said below
- ln1_gain: bfloat16 [1152], P('inner'), may hold values from 0.5 to 1.5
- ln1_bias: bfloat16 [1152], P('inner'), may hold values from -1.75 to 1.75
- w_qkv: bfloat16 [1152, 3456], P('inner'), may hold values from -0.1875 to 0.1875
- b_qv: bfloat16 [2304], P('inner'), may hold values from -3 to 3
- w_attn_out: bfloat16 [1152, 1152], P('inner'), may hold values from -0.75 to 0.75
- b_attn_out: bfloat16 [1152], P('inner'), may hold values from -1.75 to 1.75
- ln2_gain: bfloat16 [1152], P('inner'), may hold values from 0.5 to 1.5
- ln2_bias: bfloat16 [1152], P('inner'), may hold values from -1.75 to 1.75
- w_mlp_in: bfloat16 [1152, 4304], P('inner'), may hold values from -0.1875 to 0.1875
- b_mlp_in: bfloat16 [4304], P('inner'), may hold values from -3 to 3
- w_mlp_out: bfloat16 [4304, 1152], P('inner'), may hold values from -0.09375 to 0.09375
- b_mlp_out: bfloat16 [1152], P('inner'), may hold values from -1.75 to 1.75
- cotangent: bfloat16 [32, 4, 256, 1152], P(('inner', 'outer')), may hold values from -6 to 6
Outputs:
- block_out: bfloat16 [32, 4, 256, 1152], P(('inner', 'outer'))
- grad_images: bfloat16 [32, 4, 256, 1152], P(('inner', 'outer'))
- grad_ln1_gain: float32 [1152], P('inner')
- grad_ln1_bias: float32 [1152], P('inner')
- grad_w_qkv: float32 [1152, 3456], P('inner')
- grad_b_qv: float32 [2304], P('inner')
- grad_w_attn_out: float32 [1152, 1152], P('inner')
- grad_b_attn_out: float32 [1152], P('inner')
- grad_ln2_gain: float32 [1152], P('inner')
- grad_ln2_bias: float32 [1152], P('inner')
- grad_w_mlp_in: float32 [1152, 4304], P('inner')
- grad_b_mlp_in: float32 [4304], P('inner')
- grad_w_mlp_out: float32 [4304, 1152], P('inner')
- grad_b_mlp_out: float32 [1152], P('inner')
Inputs may be any that keep to these rules, and one draw needn't show every extreme that they name: `counts`: each device's images fill its slots from the first one on; some device holds 4.
All inputs are finite; a program needn't handle non-finite values.
Results may differ from a plain program's by a relative error of at most 0.013.
Values may be sent and summed in bfloat16 or wider, within the bound.
No kernel may reach another device: no remote copies, remote signals or barrier semaphores. Data moves between devices by JAX's collectives and lax.ppermute only.
A program may use at most 320 MiB of HBM per device.

v0:
```python
import math

import jax
import jax.numpy as jnp
from jax import lax
from jax.sharding import PartitionSpec as P

HEADS = 16
HEAD_DIM = 72
MICRO = 2


epsilon = 1e-06
tanh_coef = 0.7978845608028654
cubic_coef = 0.044715


def norm_parts(rows, gain, shift):
    mean_row = jnp.mean(rows, -1, keepdims=True)
    centered = rows - mean_row
    inv_std = lax.rsqrt(jnp.mean(centered * centered, -1, keepdims=True) + epsilon)
    unit_rows = centered * inv_std
    return (unit_rows * gain + shift, unit_rows, inv_std)


def norm_back(grad_normed, unit_rows, inv_std, gain):
    grad_unit = grad_normed * gain
    return inv_std * (
        grad_unit
        - jnp.mean(grad_unit, -1, keepdims=True)
        - unit_rows * jnp.mean(grad_unit * unit_rows, -1, keepdims=True)
    )


def gelu_parts(pre_act):
    tangent = jnp.tanh(tanh_coef * (pre_act + cubic_coef * pre_act * pre_act * pre_act))
    activated = 0.5 * pre_act * (1.0 + tangent)
    derivative = 0.5 * (1.0 + tangent) + 0.5 * pre_act * (1.0 - tangent * tangent) * tanh_coef * (
        1.0 + 3.0 * cubic_coef * pre_act * pre_act
    )
    return (activated, derivative)


def matmul(left, right):
    return jnp.dot(left, right, preferred_element_type=jnp.float32)


def outer_sum(left, right):
    return lax.dot_general(
        left, right, (((0,), (0,)), ((), ())), preferred_element_type=jnp.float32
    )


def times_rows(left, right):
    return lax.dot_general(
        left, right, (((1,), (1,)), ((), ())), preferred_element_type=jnp.float32
    )


def per_device(
    images,
    counts,
    ln1_gain,
    ln1_bias,
    w_qkv,
    b_qv,
    w_attn_out,
    b_attn_out,
    ln2_gain,
    ln2_bias,
    w_mlp_in,
    b_mlp_in,
    w_mlp_out,
    b_mlp_out,
    cotangent,
):
    shards = (
        ln1_gain,
        ln1_bias,
        w_qkv,
        b_qv,
        w_attn_out,
        b_attn_out,
        ln2_gain,
        ln2_bias,
        w_mlp_in,
        b_mlp_in,
        w_mlp_out,
        b_mlp_out,
    )
    slot_count = images.shape[1] // MICRO
    length = images.shape[2]
    model_width = images.shape[3]
    rows = slot_count * length
    score_scale = 1.0 / math.sqrt(HEAD_DIM)

    def split_heads(tensor):
        return tensor.reshape(slot_count, length, HEADS, HEAD_DIM)

    outputs = []
    input_grads = []
    totals = None
    for micro_step in range(MICRO):
        full = (
            lax.all_gather(shards[0], "inner", axis=0, tiled=True),
            lax.all_gather(shards[1], "inner", axis=0, tiled=True),
            lax.all_gather(shards[2], "inner", axis=0, tiled=True),
            lax.all_gather(shards[3], "inner", axis=0, tiled=True),
            lax.all_gather(shards[4], "inner", axis=0, tiled=True),
            lax.all_gather(shards[5], "inner", axis=0, tiled=True),
            lax.all_gather(shards[6], "inner", axis=0, tiled=True),
            lax.all_gather(shards[7], "inner", axis=0, tiled=True),
            lax.all_gather(shards[8], "inner", axis=0, tiled=True),
            lax.all_gather(shards[9], "inner", axis=0, tiled=True),
            lax.all_gather(shards[10], "inner", axis=0, tiled=True),
            lax.all_gather(shards[11], "inner", axis=0, tiled=True),
        )
        gain_one = full[0].astype(jnp.float32)
        shift_one = full[1].astype(jnp.float32)
        whole_qkv = full[2]
        qv_bias = full[3].astype(jnp.float32)
        whole_attn = full[4]
        bias_attn = full[5].astype(jnp.float32)
        gain_two = full[6].astype(jnp.float32)
        shift_two = full[7].astype(jnp.float32)
        whole_up = full[8]
        bias_up = full[9].astype(jnp.float32)
        whole_down = full[10]
        bias_down = full[11].astype(jnp.float32)
        start = micro_step * slot_count
        source = (
            images[0, start : start + slot_count].reshape(rows, model_width).astype(jnp.float32)
        )
        slot_ids = start + jnp.arange(slot_count, dtype=jnp.int32)
        live = (slot_ids < counts[0]).astype(jnp.float32)
        live_rows = jnp.repeat(live, length)[:, None]
        normed_one, unit_one, inv_one = norm_parts(source, gain_one, shift_one)
        normed_low = normed_one.astype(jnp.bfloat16)
        projected = matmul(normed_low, whole_qkv)
        queries = (projected[:, :model_width] + qv_bias[:model_width]).astype(jnp.bfloat16)
        key_rows = projected[:, model_width : 2 * model_width].astype(jnp.bfloat16)
        value_rows = (projected[:, 2 * model_width :] + qv_bias[model_width:]).astype(jnp.bfloat16)
        query_heads = split_heads(queries)
        key_heads = split_heads(key_rows)
        value_heads = split_heads(value_rows)
        scores = (
            jnp.einsum(
                "sqhd,skhd->shqk", query_heads, key_heads, preferred_element_type=jnp.float32
            )
            * score_scale
        )
        highest_score = jnp.max(scores, -1, keepdims=True)
        exponent = jnp.exp(scores - highest_score)
        total_exp = jnp.sum(exponent, -1, keepdims=True)
        attn_probs = exponent / total_exp
        log_total = highest_score + jnp.log(total_exp)
        attended = jnp.einsum(
            "shqk,skhd->sqhd",
            attn_probs.astype(jnp.bfloat16),
            value_heads,
            preferred_element_type=jnp.float32,
        )
        attended = attended.reshape(rows, model_width).astype(jnp.bfloat16)
        hidden = source + matmul(attended, whole_attn) + bias_attn
        normed_two, unit_two, inv_two = norm_parts(hidden, gain_two, shift_two)
        normed_two_low = normed_two.astype(jnp.bfloat16)
        pre_act = matmul(normed_two_low, whole_up) + bias_up
        activated, derivative = gelu_parts(pre_act)
        act_low = activated.astype(jnp.bfloat16)
        result = hidden + matmul(act_low, whole_down) + bias_down
        outputs.append(
            (result * live_rows).astype(jnp.bfloat16).reshape(slot_count, length, model_width)
        )
        grad_out = (
            cotangent[0, start : start + slot_count].reshape(rows, model_width).astype(jnp.float32)
            * live_rows
        )
        grad_out_low = grad_out.astype(jnp.bfloat16)
        grad_down = outer_sum(act_low, grad_out_low)
        grad_bias_down = jnp.sum(grad_out, 0)
        grad_pre = (times_rows(grad_out_low, whole_down) * derivative).astype(jnp.bfloat16)
        grad_up = outer_sum(normed_two_low, grad_pre)
        grad_bias_up = jnp.sum(grad_pre.astype(jnp.float32), 0)
        grad_normed_two = times_rows(grad_pre, whole_up)
        grad_gain_two = jnp.sum(grad_normed_two * unit_two, 0)
        grad_shift_two = jnp.sum(grad_normed_two, 0)
        grad_hidden = grad_out + norm_back(grad_normed_two, unit_two, inv_two, gain_two)
        grad_branch = grad_hidden.astype(jnp.bfloat16)
        grad_attn = outer_sum(attended, grad_branch)
        grad_bias_attn = jnp.sum(grad_branch.astype(jnp.float32), 0)
        grad_attended = split_heads(times_rows(grad_branch, whole_attn).astype(jnp.bfloat16))
        again = (
            jnp.einsum(
                "sqhd,skhd->shqk", query_heads, key_heads, preferred_element_type=jnp.float32
            )
            * score_scale
        )
        probs_again = jnp.exp(again - log_total)
        grad_values = jnp.einsum(
            "shqk,sqhd->skhd",
            probs_again.astype(jnp.bfloat16),
            grad_attended,
            preferred_element_type=jnp.float32,
        ).astype(jnp.bfloat16)
        grad_probs = jnp.einsum(
            "sqhd,skhd->shqk", grad_attended, value_heads, preferred_element_type=jnp.float32
        )
        row_dot = jnp.sum(grad_probs * probs_again, -1, keepdims=True)
        grad_scores = (probs_again * (grad_probs - row_dot)).astype(jnp.bfloat16)
        grad_queries = (
            jnp.einsum(
                "shqk,skhd->sqhd", grad_scores, key_heads, preferred_element_type=jnp.float32
            )
            * score_scale
        ).astype(jnp.bfloat16)
        grad_keys = (
            jnp.einsum(
                "shqk,sqhd->skhd", grad_scores, query_heads, preferred_element_type=jnp.float32
            )
            * score_scale
        ).astype(jnp.bfloat16)
        grad_qkv = jnp.concatenate(
            [
                grad_queries.reshape(rows, model_width),
                grad_keys.reshape(rows, model_width),
                grad_values.reshape(rows, model_width),
            ],
            axis=1,
        )
        grad_whole_qkv = outer_sum(normed_low, grad_qkv)
        grad_qv_bias = jnp.concatenate(
            [
                jnp.sum(grad_qkv[:, :model_width].astype(jnp.float32), 0),
                jnp.sum(grad_qkv[:, 2 * model_width :].astype(jnp.float32), 0),
            ]
        )
        grad_normed_one = times_rows(grad_qkv, whole_qkv)
        grad_gain_one = jnp.sum(grad_normed_one * unit_one, 0)
        grad_shift_one = jnp.sum(grad_normed_one, 0)
        grad_source = grad_hidden + norm_back(grad_normed_one, unit_one, inv_one, gain_one)
        input_grads.append(
            grad_source.astype(jnp.bfloat16).reshape(slot_count, length, model_width)
        )
        grads = (
            grad_gain_one,
            grad_shift_one,
            grad_whole_qkv,
            grad_qv_bias,
            grad_attn,
            grad_bias_attn,
            grad_gain_two,
            grad_shift_two,
            grad_up,
            grad_bias_up,
            grad_down,
            grad_bias_down,
        )
        totals = grads if totals is None else jax.tree.map(jnp.add, tuple(totals), tuple(grads))
    totals = (
        lax.psum_scatter(totals[0], "inner", scatter_dimension=0, tiled=True),
        lax.psum_scatter(totals[1], "inner", scatter_dimension=0, tiled=True),
        lax.psum_scatter(totals[2], "inner", scatter_dimension=0, tiled=True),
        lax.psum_scatter(totals[3], "inner", scatter_dimension=0, tiled=True),
        lax.psum_scatter(totals[4], "inner", scatter_dimension=0, tiled=True),
        lax.psum_scatter(totals[5], "inner", scatter_dimension=0, tiled=True),
        lax.psum_scatter(totals[6], "inner", scatter_dimension=0, tiled=True),
        lax.psum_scatter(totals[7], "inner", scatter_dimension=0, tiled=True),
        lax.psum_scatter(totals[8], "inner", scatter_dimension=0, tiled=True),
        lax.psum_scatter(totals[9], "inner", scatter_dimension=0, tiled=True),
        lax.psum_scatter(totals[10], "inner", scatter_dimension=0, tiled=True),
        lax.psum_scatter(totals[11], "inner", scatter_dimension=0, tiled=True),
    )
    summed = lax.psum(
        (
            totals[0],
            totals[1],
            totals[2],
            totals[3],
            totals[4],
            totals[5],
            totals[6],
            totals[7],
            totals[8],
            totals[9],
            totals[10],
            totals[11],
        ),
        "outer",
    )
    block_out = jnp.concatenate(outputs, 0)[None]
    grad_images = jnp.concatenate(input_grads, 0)[None]
    return (
        block_out,
        grad_images,
        summed[0],
        summed[1],
        summed[2],
        summed[3],
        summed[4],
        summed[5],
        summed[6],
        summed[7],
        summed[8],
        summed[9],
        summed[10],
        summed[11],
    )


def solution(mesh):
    return jax.shard_map(
        per_device,
        mesh=mesh,
        in_specs=(
            P(("inner", "outer"), None, None, None),
            P(("inner", "outer")),
            P("inner"),
            P("inner"),
            P("inner", None),
            P("inner"),
            P("inner", None),
            P("inner"),
            P("inner"),
            P("inner"),
            P("inner", None),
            P("inner"),
            P("inner", None),
            P("inner"),
            P(("inner", "outer"), None, None, None),
        ),
        out_specs=(
            P(("inner", "outer"), None, None, None),
            P(("inner", "outer"), None, None, None),
            P("inner"),
            P("inner"),
            P("inner", None),
            P("inner"),
            P("inner", None),
            P("inner"),
            P("inner"),
            P("inner"),
            P("inner", None),
            P("inner"),
            P("inner", None),
            P("inner"),
        ),
        check_vma=False,
    )
```

profile of v0, /device:TPU:0, one launch (start us, length us, event | category | flops | bytes accessed | tf_op | source)
XLA Modules:
  0.0 1286.3 jit_solution(782274486469420072)
XLA Ops:
  11.5 2.5 slice_convert_fusion.3
  24.8 4.2 all-reduce.20
  30.3 3.6 fusion.43
  33.9 2.0 add_convert_fusion.5
  35.9 8.2 fusion.81
  44.2 6.9 fusion.82
  51.2 3.7 reshape.338
  56.5 3.9 slice.99
  60.4 7.9 fusion.37
  68.2 5.0 reshape.340
  73.2 2.6 copy.104
  75.8 5.0 reshape.341
  80.8 2.6 copy.105
  83.4 5.1 reshape.339
  88.5 2.6 copy.106
  91.1 5.0 reshape.336
  96.1 2.8 copy.98
  98.9 5.7 reshape.337
  104.6 3.0 copy.96
  112.4 2.0 fusion.63
  120.8 2.4 fusion.64
  125.8 4.0 fusion.80
  131.9 2.1 fusion.79
  137.2 11.2 convolution_add_fusion.4
  148.4 16.3 %convert_reduce_fusion = (f32[4304]{0:T(1024)}, bf16[512,4304]{0,1:T(8,128)(2,1)S(1)}) fusion(f32[512,4304]{0,1:T(8,128)} %convolution_add_fusion.4, bf16[512,1152]{1,0:T(8,128)(2,1)} %get-tuple-element.82, bf16[4304,1152]{1,0:T(8,128)(2,1)} %all-gather.12.cloned.1.call-done), kind=kOutput, calls=%fused_computation.22 | convolution fusion | flops 5123477504 | bytes 24335168 | tf_op jit(solution)/shard_map/dot_general | solution.py:55
  164.7 12.3 fusion.83
  177.0 12.0 convolution_add_fusion.5
  189.0 17.4 %convert_reduce_fusion.1 = (f32[4304]{0:T(1024)}, bf16[512,4304]{0,1:T(8,128)(2,1)}) fusion(f32[512,4304]{0,1:T(8,128)} %convolution_add_fusion.5, bf16[512,1152]{1,0:T(8,128)(2,1)S(1)} %copy-done.46, bf16[4304,1152]{1,0:T(8,128)(2,1)} %all-gather.12.cloned.1.call-done), kind=kOutput, calls=%fused_computation.23 | convolution fusion | flops 5123477504 | bytes 24335168 | tf_op jit(solution)/shard_map/dot_general | solution.py:55
  206.4 14.5 %multiply_reduce_fusion.7 = (f32[1152]{0:T(1024)}, f32[512]{0:T(512)S(1)}, f32[512]{0:T(512)S(1)}, f32[1152]{0:T(1024)}, f32[1152]{0:T(1024)}, /*index=5*/f32[51...) fusion(f32[512,1152]{1,0:T(8,128)S(1)} %copy-done.6, f32[512]{0:T(512)S(1)} %copy-done.96, ...), kind=kOutput, calls=%fused_computation.87 | convolution fusion | flops 5087815680 | bytes 23800320 | tf_op jit(solution)/shard_map/dot_general | solution.py:55
  220.9 5.4 convert_reduce_fusion.3
  226.4 4.1 fusion.67
  232.4 4.7 reshape.342
  237.1 3.0 copy.110
  240.1 7.7 convolution_add_fusion.3
  248.0 6.9 convert_reduce_fusion.6
  254.9 2.9 convolution_convert_fusion
  257.8 5.7 reshape.343
  263.5 4.1 copy.122
  267.7 2.6 copy.120
  270.6 5.9 convert_reduce_fusion.4
  278.0 2.3 multiply_reduce_fusion
  280.3 2.4 multiply_convert_fusion.2
  289.8 2.3 multiply_reduce_fusion.1
  292.1 2.6 multiply_convert_fusion.3
  302.6 7.9 fusion.85
  310.5 11.3 convolution_add_fusion.2
  322.4 15.6 %fusion.76 = f32[1152,4304]{1,0:T(8,128)} fusion(bf16[512,4304]{0,1:T(8,128)(2,1)} %get-tuple-element.121, f32[512,1152]{1,0:T(8,128)} %copy-done.5, f32[1152]{0:T(1024)S(1)} %copy-done.63, f32[1152]{0:T(1024)S(1)} %convert_element_type.258, f32[512]{0:T(512)S(1)} %copy-done.97, f32[512]{0:T(512)S(1)} %copy-done.87), kind=kOutput, calls=%fused_computation.183 | convolution fusion | flops 5080154112 | bytes 26612736 | tf_op jit(solution)/shard_map/dot_general | solution.py:49
  338.0 21.7 %convolution_add_fusion.1 = f32[1152,4304]{1,0:T(8,128)} fusion(f32[1152,4304]{1,0:T(8,128)} %fusion.76, bf16[512,4304]{0,1:T(8,128)(2,1)} %copy-done.40, f32[512,1152]{1,0:T(8,128)S(1)} %get-tuple-element.101, f32[512]{0:T(512)S(1)} %copy-done.68, f32[512]{0:T(512)S(1)} %copy-done.66, f32[1152]{0:T(1024)S(1)} %copy-done.63, f32[1152]{0:T(1024)S(1)} %convert_element_type.258), kind=kOutput, calls=%fused_computation.1 | convolution fusion | flops 5085112320 | bytes 46445568 | tf_op jit(solution)/shard_map/dot_general | solution.py:49
  361.0 16.7 %fusion.77 = f32[4304,1152]{1,0:T(8,128)} fusion(bf16[512,1152]{1,0:T(8,128)(2,1)S(1)} %copy-done.47, f32[512,4304]{0,1:T(8,128)} %convolution_add_fusion.5), kind=kOutput, calls=%fused_computation.184 | convolution fusion | flops 5097037824 | bytes 29827072 | tf_op jit(solution)/shard_map/dot_general | solution.py:49
  377.7 25.1 %convolution_add_fusion = f32[4304,1152]{1,0:T(8,128)} fusion(f32[4304,1152]{1,0:T(8,128)} %fusion.77, bf16[512,1152]{1,0:T(8,128)(2,1)S(1)} %copy-done.39, f32[512,4304]{0,1:T(8,128)} %convolution_add_fusion.4), kind=kOutput, calls=%fused_computation | convolution fusion | flops 5101996032 | bytes 49659904 | tf_op jit(solution)/shard_map/dot_general | solution.py:49
  402.8 31.3 %fusion = f32[2176,1152]{1,0:T(8,128)} fusion(f32[4304,1152]{1,0:T(8,128)} %convolution_add_fusion), kind=kCustom, calls=%all-reduce-scatter | all-reduce-scatter fusion | flops 5013505 | bytes 29860352
  434.9 2.0 collective-permute-start
  437.9 24.3 %concatenate.24 = f32[2200,1152]{1,0:T(8,128)} concatenate(f32[24,1152]{1,0:T(8,128)S(1)} %collective-permute-done, f32[2176,1152]{1,0:T(8,128)} %fusion), dimensions={0} | concatenate | bytes 20275200
  462.2 8.4 constant_dynamic-slice_fusion
  474.2 10.7 fusion.84
  485.0 11.9 multiply_reduce_fusion.9
  496.9 4.0 all-reduce.19
  501.5 81.8 %all-reduce.17 = (f32[576]{0:T(1024)}, f32[576]{0:T(1024)}, f32[1152]{0:T(1024)}, f32[576]{0:T(1024)}, f32[576]{0:T(1024)}, /*index=5*/f32[576]{0:T(1024)}, f32[2152]{0:T(1024)}, f32[576]{0:T(1024)}) all-reduce(f32[576]{0:T(1024)S(1)} %dynamic-slice.8, f32[576]{0:T(1024)S(1)} %dynamic-slice.10, ...), channel_id=1, replica_groups=mesh['inner'=2,'outer'=16] {'outer'}, use_global_device_ids=true, to_apply=%region_25.0 | all-reduce | flops 6760 | bytes 54080 | tf_op jit(solution)/shard_map/psum | solution.py:273
  583.4 12.2 fusion.36
  595.6 12.4 fusion.35
  614.7 641.5 %all-reduce.23.cloned.1.call-done = (f32[576,3456]{1,0:T(8,128)}, f32[576,1152]{1,0:T(8,128)}, f32[576,4304]{1,0:T(8,128)}, f32[2152,1152]{1,0:T(8,128)}) async-done(((f32[576,3456]{1,0:T(8,128)}, f32[576,1152]{1,0:T(8,128)}, f32[576,4304]{1,0:T(8,128)}, f32[2152,1152]{1,0:T(8,128)}), (f32[576,3456]{1,0:T(8,128)}, f32[576,1152]{1,0:T(8,128)}, f32[576,4304]{1,0:T(8,128)}, ...) | async-done | bytes 30449680 | tf_op jit(solution)/shard_map/psum | solution.py:273
  1256.3 8.0 copy.187
  1267.0 3.9 copy.189
  1270.9 8.4 copy.190
  (382 shorter events, 67.8 us)
Async XLA Ops:
  7.2 28.8 %all-gather.6.cloned.1.call-start = ((), (), s32[]{:S(2)}) async-start(), calls=%async_computation.3 | async-start | bytes 11943936 | tf_op jit(solution)/shard_map/all_gather | solution.py:107
  7.9 117.9 %all-gather.8.cloned.1.call-start = ((), (), s32[]{:S(2)}) async-start(), calls=%async_computation.4 | async-start | bytes 3981312 | tf_op jit(solution)/shard_map/all_gather | solution.py:109
  8.7 128.6 %all-gather.10.cloned.1.call-start = ((), (), s32[]{:S(2)}) async-start(), calls=%async_computation.5 | async-start | bytes 15040512 | tf_op jit(solution)/shard_map/all_gather | solution.py:113
  9.4 139.0 %all-gather.12.cloned.1.call-start = ((), (), s32[]{:S(2)}) async-start(), calls=%async_computation.6 | async-start | bytes 14874624 | tf_op jit(solution)/shard_map/all_gather | solution.py:115
  10.0 460.6 %reduce-scatter.8.cloned.1.call-start = ((), (), s32[]{:S(2)}) async-start(), calls=%async_computation.8 | async-start | bytes 7962624 | tf_op jit(solution)/shard_map/reduce_scatter | solution.py:264
  13.9 6.5 copy-start.105
  13.9 9.1 copy-start.110
  14.0 9.4 copy-start.111
  14.0 9.6 copy-start.112
  14.0 9.8 copy-start.113
  14.0 10.1 copy-start.114
  14.0 10.3 copy-start.115
  14.0 10.5 copy-start.102
  16.7 6.3 copy-start.108
  16.8 17.0 %copy-start.82 = (f32[1,2,2,128]{3,1,2,0:T(2,128)}, f32[1,2,2,128]{3,1,2,0:T(2,128)S(1)}, u32[]{:S(2)}) copy-start(f32[1,2,2,128]{3,1,2,0:T(2,128)S(1)} %copy.164) | copy-start | bytes 6148
  17.3 16.6 %copy-start.79 = (f32[1,2,2,128]{3,1,2,0:T(2,128)}, f32[1,2,2,128]{3,1,2,0:T(2,128)S(1)}, u32[]{:S(2)}) copy-start(f32[1,2,2,128]{3,1,2,0:T(2,128)S(1)} %copy.160) | copy-start | bytes 6148
  35.9 8.2 copy-start.30
  35.9 8.2 copy-start.116
  44.1 6.9 copy-start.33
  54.9 5.5 copy-start.71
  54.9 5.5 copy-start.72
  56.5 51.1 %copy-start.19 = (bf16[2,256,16,72]{1,3,2,0:T(8,128)(2,1)}, bf16[2,256,16,72]{1,3,2,0:T(8,128)(2,1)S(1)}, u32[]{:S(2)}) copy-start(bf16[2,256,16,72]{1,3,2,0:T(8,128)(2,1)S(1)} %copy.97) | copy-start | bytes 3538948
  134.0 204.0 %copy-start.4 = (f32[512,1152]{1,0:T(8,128)}, f32[512,1152]{1,0:T(8,128)S(1)}, u32[]{:S(2)}) copy-start(f32[512,1152]{1,0:T(8,128)S(1)} %get-tuple-element.101) | copy-start | bytes 7077892
  164.7 12.3 copy-start.40
  164.7 12.3 copy-start.6
  164.7 12.3 copy-start.76
  164.7 12.3 copy-start.86
  164.7 12.3 copy-start.96
  177.0 12.0 copy-start.46
  189.0 17.4 %copy-start.42 = (f32[512,1152]{1,0:T(8,128)S(1)}, f32[512,1152]{1,0:T(8,128)}, u32[]{:S(2)}) copy-start(f32[512,1152]{1,0:T(8,128)} %fusion.83) | copy-start | bytes 7077892
  189.0 17.4 %copy-start.65 = (f32[512]{0:T(512)S(1)}, f32[512]{0:T(512)}, u32[]{:S(2)}) copy-start(f32[512]{0:T(512)} %copy-done.64) | copy-start | bytes 6148
  189.0 17.4 %copy-start.67 = (f32[512]{0:T(512)S(1)}, f32[512]{0:T(512)}, u32[]{:S(2)}) copy-start(f32[512]{0:T(512)} %add_rsqrt_fusion) | copy-start | bytes 6148
  206.4 14.5 %copy-start.8 = (bf16[1,4,256,1152]{3,2,1,0:T(8,128)(2,1)S(1)}, bf16[1,4,256,1152]{3,2,1,0:T(8,128)(2,1)}, u32[]{:S(2)}) copy-start(bf16[1,4,256,1152]{3,2,1,0:T(8,128)(2,1)} %param.29) | copy-start | bytes 7077892
  206.4 14.6 %copy-start.80 = (f32[1,2,2,128]{3,1,2,0:T(2,128)S(1)}, f32[1,2,2,128]{3,1,2,0:T(2,128)}, u32[]{:S(2)}) copy-start(f32[1,2,2,128]{3,1,2,0:T(2,128)} %copy-done.79) | copy-start | bytes 6148
  206.4 14.6 %copy-start.83 = (f32[1,2,2,128]{3,1,2,0:T(2,128)S(1)}, f32[1,2,2,128]{3,1,2,0:T(2,128)}, u32[]{:S(2)}) copy-start(f32[1,2,2,128]{3,1,2,0:T(2,128)} %copy-done.82) | copy-start | bytes 6148
  247.8 222.8 %reduce-scatter.6.cloned.1.call-start = ((), (), s32[]{:S(2)}) async-start(), calls=%async_computation.7 | async-start | bytes 23887872 | tf_op jit(solution)/shard_map/reduce_scatter | solution.py:262
  248.0 6.9 copy-start.10
  248.0 6.9 copy-start.18
  270.3 7.7 slice-start.2
  270.6 7.4 slice-start.3
  282.7 7.0 slice-start
  300.4 10.1 copy-start.32
  302.6 7.9 copy-start.31
  321.8 16.2 %copy-start.66 = (f32[512]{0:T(512)S(1)}, f32[512]{0:T(512)}, u32[]{:S(2)}) copy-start(f32[512]{0:T(512)} %copy-done.64) | copy-start | bytes 6148
  321.8 16.2 %copy-start.68 = (f32[512]{0:T(512)S(1)}, f32[512]{0:T(512)}, u32[]{:S(2)}) copy-start(f32[512]{0:T(512)} %add_rsqrt_fusion) | copy-start | bytes 6148
  321.8 148.8 %reduce-scatter.10.cloned.1.call-start = ((), (), s32[]{:S(2)}) async-start(), calls=%async_computation.9 | async-start | bytes 30081024 | tf_op jit(solution)/shard_map/reduce_scatter | solution.py:268
  359.7 18.0 %copy-start.39 = (bf16[512,1152]{1,0:T(8,128)(2,1)S(1)}, bf16[512,1152]{1,0:T(8,128)(2,1)}, u32[]{:S(2)}) copy-start(bf16[512,1152]{1,0:T(8,128)(2,1)} %get-tuple-element.82) | copy-start | bytes 3538948
  359.7 896.5 %all-reduce.23.cloned.1.call-start = ((), (), s32[]{:S(2)}) async-start(), calls=%async_computation.10 | async-start | bytes 61120512 | tf_op jit(solution)/shard_map/psum | solution.py:273
  434.9 3.0 collective-permute-start
  474.1 10.8 copy-start.3
  474.1 10.8 copy-start.52
  474.1 10.8 copy-start.62
  474.1 10.8 copy-start.89
  474.1 10.8 copy-start.91
  474.1 10.8 copy-start.93
  474.2 10.8 copy-start.95
  484.9 11.9 copy-start.43
  485.0 98.4 %copy-start.84 = (f32[1,2,2,128]{3,1,2,0:T(2,128)S(1)}, f32[1,2,2,128]{3,1,2,0:T(2,128)}, u32[]{:S(2)}) copy-start(f32[1,2,2,128]{3,1,2,0:T(2,128)} %copy-done.82) | copy-start | bytes 6148
  583.3 12.2 copy-start.7
  583.4 12.2 copy-start.81
  595.6 14.1 %copy-start.44 = (f32[512,1152]{1,0:T(8,128)S(1)}, f32[512,1152]{1,0:T(8,128)}, u32[]{:S(2)}) copy-start(f32[512,1152]{1,0:T(8,128)} %copy-done.43) | copy-start | bytes 7077892
  595.6 14.1 %copy-start.45 = (f32[512,1152]{1,0:T(8,128)S(1)}, f32[512,1152]{1,0:T(8,128)}, u32[]{:S(2)}) copy-start(f32[512,1152]{1,0:T(8,128)} %get-tuple-element.111) | copy-start | bytes 7077892
  1256.2 8.0 copy-start.41
  1256.2 10.8 copy-start.27
  (66 other events, 178.7 us)
Sparse Core Ops, SparseCore 0:
  9.5 21.9 all-gather.5
  33.1 12.5 all-gather.7
  47.3 23.3 all-gather.9
  72.1 23.2 all-gather.11
  247.9 15.6 reduce-scatter.7
  321.9 27.3 reduce-scatter.5
  359.8 31.1 reduce-scatter.9
  470.7 785.4 all-reduce.22
where the time goes:
time: 1290 us
  waiting for transfers between devices  645 us (50%)
  matrix products  297 us (23%)
  local copies, waits for them, and re-layouts  158 us (12%)
  blocking collectives  123 us (10%)
  other arithmetic  41.1 us (3%)
  between operations  20.8 us (2%)
    psum x1, waiting for transfers between devices, per_device(): lax.psum((totals[0], totals[1], totals[2], totals[3], totals[4], totals[5...  642 us
    dot_general x8, matrix products, outer_sum(): lax.dot_general(left, right, (((0,), (0,)), ((), ())), preferred_element_...  110 us
    dot_general x8, matrix products, times_rows(): lax.dot_general(left, right, (((1,), (1,)), ((), ())), preferred_element_...  87.9 us
    psum x1, blocking collectives, per_device(): lax.psum((totals[0], totals[1], totals[2], totals[3], totals[4], totals[5...  81.8 us
    unnamed x293, local copies, waits for them, and re-layouts  79.3 us
    dot_general x8, matrix products, matmul(): return jnp.dot(left, right, preferred_element_type=jnp.float32)  68.8 us
    reshape x16, local copies, waits for them, and re-layouts, split_heads(): return tensor.reshape(slot_count, length, HEADS, HEAD_DIM)  62.2 us
    unnamed x3, blocking collectives  39.5 us
  transfers between devices with their start and end apart: 9, of which 2 were waited for; matrix products, arithmetic and copies ran while one was open for 30% of the time, Pallas kernels for 0%

commit v1 on v0

v1 whole, which is shorter than its diff:
```python
import functools
import math

import jax
import jax.numpy as jnp
from jax import lax
from jax.sharding import PartitionSpec as P

HEADS = 16
HEAD_DIM = 72


epsilon = 1e-06
tanh_coef = 0.7978845608028654
cubic_coef = 0.044715


def norm_parts(rows, gain, shift):
    mean_row = jnp.mean(rows, -1, keepdims=True)
    centered = rows - mean_row
    inv_std = lax.rsqrt(jnp.mean(centered * centered, -1, keepdims=True) + epsilon)
    unit_rows = centered * inv_std
    return (unit_rows * gain + shift, unit_rows, inv_std)


def norm_back(grad_normed, unit_rows, inv_std, gain):
    grad_unit = grad_normed * gain
    return inv_std * (
        grad_unit
        - jnp.mean(grad_unit, -1, keepdims=True)
        - unit_rows * jnp.mean(grad_unit * unit_rows, -1, keepdims=True)
    )


def gelu_parts(pre_act):
    tangent = jnp.tanh(tanh_coef * (pre_act + cubic_coef * pre_act * pre_act * pre_act))
    activated = 0.5 * pre_act * (1.0 + tangent)
    derivative = 0.5 * (1.0 + tangent) + 0.5 * pre_act * (1.0 - tangent * tangent) * tanh_coef * (
        1.0 + 3.0 * cubic_coef * pre_act * pre_act
    )
    return (activated, derivative)


def matmul(left, right):
    return jnp.dot(left, right, preferred_element_type=jnp.float32)


def outer_sum(left, right):
    return lax.dot_general(
        left, right, (((0,), (0,)), ((), ())), preferred_element_type=jnp.float32
    )


def times_rows(left, right):
    return lax.dot_general(
        left, right, (((1,), (1,)), ((), ())), preferred_element_type=jnp.float32
    )


def cut(tensor, at, size):
    return lax.dynamic_slice_in_dim(tensor, at * size, size, 0)


def swap(tensor, axis, size, stride):
    return lax.ppermute(tensor, axis, [(i, i ^ stride) for i in range(size)])


def bit_of(axis, stride):
    return (lax.axis_index(axis) // stride) % 2


def pad_rows(tensor, rows):
    return tensor if tensor.shape[0] == rows else jnp.pad(tensor, ((0, rows - tensor.shape[0]), (0, 0)))


def scatter_stage(total, axis, size, stride):
    rows = -(-total.shape[0] // 16) * 16
    total = pad_rows(total, rows)
    bit = bit_of(axis, stride)
    arrived = swap(cut(total, 1 - bit, rows // 2).astype(jnp.bfloat16), axis, size, stride)
    return cut(total, bit, rows // 2) + arrived.astype(jnp.float32)


def join(own, other, bit):
    return jnp.where(bit == 0, jnp.concatenate([own, other], 0), jnp.concatenate([other, own], 0))


def gather_stage(block, axis, size, stride):
    return join(block, swap(block, axis, size, stride), bit_of(axis, stride))


def reduce_outer(total, size, order):
    if size & (size - 1):
        return lax.psum(total, "outer")
    shapes = []
    for stride in order:
        shapes.append(total.shape[0])
        total = scatter_stage(total, "outer", size, stride)
    block = total.astype(jnp.bfloat16)
    for stride, rows in zip(reversed(order), reversed(shapes)):
        block = gather_stage(block, "outer", size, stride)[:rows]
    return block.astype(jnp.float32)


def orders(size):
    strides = [1 << k for k in range(size.bit_length() - 1)]
    other = strides[1:2] + strides[:1] + strides[2:]
    return strides, other


def sum_to_owner(grad, inner, outer):
    rows = grad.shape[0] // inner
    if inner == 2:
        bit = lax.axis_index("inner")
        arrived = swap(cut(grad, 1 - bit, rows).astype(jnp.bfloat16), "inner", 2, 1)
        mine = cut(grad, bit, rows) + arrived.astype(jnp.float32)
    else:
        mine = lax.psum_scatter(grad, "inner", scatter_dimension=0, tiled=True)
    first, second = orders(outer)
    middle = (grad.shape[1] // 256) * 128
    return jnp.concatenate(
        [
            reduce_outer(mine[:, :middle], outer, first),
            reduce_outer(mine[:, middle:], outer, second),
        ],
        1,
    )


def sum_everywhere(vector, inner, outer):
    for axis, size in (("inner", inner), ("outer", outer)):
        if size & (size - 1):
            vector = lax.psum(vector, axis)
        else:
            stride = 1
            while stride < size:
                vector = vector + swap(vector, axis, size, stride)
                stride *= 2
    return vector


def whole(shard, inner):
    if inner == 2:
        return join(shard, swap(shard, "inner", 2, 1), lax.axis_index("inner"))
    return lax.all_gather(shard, "inner", axis=0, tiled=True)


def swap_small(small, shards, inner):
    if inner == 2:
        other = swap(small.reshape(1, -1), "inner", 2, 1).reshape(-1)
    every = lax.all_gather(small, "inner") if inner != 2 else None
    out = {}
    at = 0
    for k in (0, 1, 3, 5, 6, 7, 9, 11):
        size = shards[k].shape[0]
        if inner == 2:
            out[k] = join(small[at : at + size], other[at : at + size], lax.axis_index("inner"))
        else:
            out[k] = every[:, at : at + size].reshape(-1)
        at += size
    return out


def per_device(
    inner,
    outer,
    images,
    counts,
    ln1_gain,
    ln1_bias,
    w_qkv,
    b_qv,
    w_attn_out,
    b_attn_out,
    ln2_gain,
    ln2_bias,
    w_mlp_in,
    b_mlp_in,
    w_mlp_out,
    b_mlp_out,
    cotangent,
):
    shards = (
        ln1_gain,
        ln1_bias,
        w_qkv,
        b_qv,
        w_attn_out,
        b_attn_out,
        ln2_gain,
        ln2_bias,
        w_mlp_in,
        b_mlp_in,
        w_mlp_out,
        b_mlp_out,
    )
    slot_count = images.shape[1]
    length = images.shape[2]
    model_width = images.shape[3]
    rows = slot_count * length
    score_scale = 1.0 / math.sqrt(HEAD_DIM)

    def split_heads(tensor):
        return tensor.reshape(slot_count, length, HEADS, HEAD_DIM)

    small = jnp.concatenate([shards[k] for k in (0, 1, 3, 5, 6, 7, 9, 11)])
    small = swap_small(small, shards, inner)
    full = tuple(
        small[k] if k in small else whole(shards[k], inner) for k in range(12)
    )
    gain_one = full[0].astype(jnp.float32)
    shift_one = full[1].astype(jnp.float32)
    whole_qkv = full[2]
    qv_bias = full[3].astype(jnp.float32)
    whole_attn = full[4]
    bias_attn = full[5].astype(jnp.float32)
    gain_two = full[6].astype(jnp.float32)
    shift_two = full[7].astype(jnp.float32)
    whole_up = full[8]
    bias_up = full[9].astype(jnp.float32)
    whole_down = full[10]
    bias_down = full[11].astype(jnp.float32)
    start = 0
    source = (
        images[0, start : start + slot_count].reshape(rows, model_width).astype(jnp.float32)
    )
    slot_ids = start + jnp.arange(slot_count, dtype=jnp.int32)
    live = (slot_ids < counts[0]).astype(jnp.float32)
    live_rows = jnp.repeat(live, length)[:, None]
    normed_one, unit_one, inv_one = norm_parts(source, gain_one, shift_one)
    normed_low = normed_one.astype(jnp.bfloat16)
    projected = matmul(normed_low, whole_qkv)
    queries = (projected[:, :model_width] + qv_bias[:model_width]).astype(jnp.bfloat16)
    key_rows = projected[:, model_width : 2 * model_width].astype(jnp.bfloat16)
    value_rows = (projected[:, 2 * model_width :] + qv_bias[model_width:]).astype(jnp.bfloat16)
    query_heads = split_heads(queries)
    key_heads = split_heads(key_rows)
    value_heads = split_heads(value_rows)
    scores = (
        jnp.einsum(
            "sqhd,skhd->shqk", query_heads, key_heads, preferred_element_type=jnp.float32
        )
        * score_scale
    )
    highest_score = jnp.max(scores, -1, keepdims=True)
    exponent = jnp.exp(scores - highest_score)
    total_exp = jnp.sum(exponent, -1, keepdims=True)
    attn_probs = exponent / total_exp
    log_total = highest_score + jnp.log(total_exp)
    attended = jnp.einsum(
        "shqk,skhd->sqhd",
        attn_probs.astype(jnp.bfloat16),
        value_heads,
        preferred_element_type=jnp.float32,
    )
    attended = attended.reshape(rows, model_width).astype(jnp.bfloat16)
    hidden = source + matmul(attended, whole_attn) + bias_attn
    normed_two, unit_two, inv_two = norm_parts(hidden, gain_two, shift_two)
    normed_two_low = normed_two.astype(jnp.bfloat16)
    pre_act = matmul(normed_two_low, whole_up) + bias_up
    activated, derivative = gelu_parts(pre_act)
    act_low = activated.astype(jnp.bfloat16)
    result = hidden + matmul(act_low, whole_down) + bias_down
    block_out = (
        (result * live_rows).astype(jnp.bfloat16).reshape(slot_count, length, model_width)
    )
    grad_out = (
        cotangent[0, start : start + slot_count].reshape(rows, model_width).astype(jnp.float32)
        * live_rows
    )
    grad_out_low = grad_out.astype(jnp.bfloat16)
    grad_down = outer_sum(act_low, grad_out_low)
    grad_bias_down = jnp.sum(grad_out, 0)
    grad_pre = (times_rows(grad_out_low, whole_down) * derivative).astype(jnp.bfloat16)
    grad_up = outer_sum(normed_two_low, grad_pre)
    grad_bias_up = jnp.sum(grad_pre.astype(jnp.float32), 0)
    grad_normed_two = times_rows(grad_pre, whole_up)
    grad_gain_two = jnp.sum(grad_normed_two * unit_two, 0)
    grad_shift_two = jnp.sum(grad_normed_two, 0)
    grad_hidden = grad_out + norm_back(grad_normed_two, unit_two, inv_two, gain_two)
    grad_branch = grad_hidden.astype(jnp.bfloat16)
    grad_attn = outer_sum(attended, grad_branch)
    grad_bias_attn = jnp.sum(grad_branch.astype(jnp.float32), 0)
    grad_attended = split_heads(times_rows(grad_branch, whole_attn).astype(jnp.bfloat16))
    again = (
        jnp.einsum(
            "sqhd,skhd->shqk", query_heads, key_heads, preferred_element_type=jnp.float32
        )
        * score_scale
    )
    probs_again = jnp.exp(again - log_total)
    grad_values = jnp.einsum(
        "shqk,sqhd->skhd",
        probs_again.astype(jnp.bfloat16),
        grad_attended,
        preferred_element_type=jnp.float32,
    ).astype(jnp.bfloat16)
    grad_probs = jnp.einsum(
        "sqhd,skhd->shqk", grad_attended, value_heads, preferred_element_type=jnp.float32
    )
    row_dot = jnp.sum(grad_probs * probs_again, -1, keepdims=True)
    grad_scores = (probs_again * (grad_probs - row_dot)).astype(jnp.bfloat16)
    grad_queries = (
        jnp.einsum(
            "shqk,skhd->sqhd", grad_scores, key_heads, preferred_element_type=jnp.float32
        )
        * score_scale
    ).astype(jnp.bfloat16)
    grad_keys = (
        jnp.einsum(
            "shqk,sqhd->skhd", grad_scores, query_heads, preferred_element_type=jnp.float32
        )
        * score_scale
    ).astype(jnp.bfloat16)
    grad_qkv = jnp.concatenate(
        [
            grad_queries.reshape(rows, model_width),
            grad_keys.reshape(rows, model_width),
            grad_values.reshape(rows, model_width),
        ],
        axis=1,
    )
    grad_whole_qkv = outer_sum(normed_low, grad_qkv)
    grad_qv_bias = jnp.concatenate(
        [
            jnp.sum(grad_qkv[:, :model_width].astype(jnp.float32), 0),
            jnp.sum(grad_qkv[:, 2 * model_width :].astype(jnp.float32), 0),
        ]
    )
    grad_normed_one = times_rows(grad_qkv, whole_qkv)
    grad_gain_one = jnp.sum(grad_normed_one * unit_one, 0)
    grad_shift_one = jnp.sum(grad_normed_one, 0)
    grad_source = grad_hidden + norm_back(grad_normed_one, unit_one, inv_one, gain_one)
    grad_images = (
        grad_source.astype(jnp.bfloat16).reshape(slot_count, length, model_width)
    )
    grads = (
        grad_gain_one,
        grad_shift_one,
        grad_whole_qkv,
        grad_qv_bias,
        grad_attn,
        grad_bias_attn,
        grad_gain_two,
        grad_shift_two,
        grad_up,
        grad_bias_up,
        grad_down,
        grad_bias_down,
    )
    vectors = (0, 1, 3, 5, 6, 7, 9, 11)
    flat = jnp.concatenate([grads[k] for k in vectors])
    length_all = flat.shape[0]
    flat = jnp.pad(flat, (0, -length_all % 1024)).reshape(8, -1)
    flat = sum_everywhere(flat, inner, outer).reshape(-1)
    summed = {}
    at = 0
    for k in vectors:
        rows_here = grads[k].shape[0]
        part = rows_here // inner
        summed[k] = lax.dynamic_slice_in_dim(
            flat[at : at + rows_here], lax.axis_index("inner") * part, part, 0
        )
        at += rows_here
    for k in (10, 8, 4, 2):
        summed[k] = sum_to_owner(grads[k], inner, outer)
    return (block_out[None], grad_images[None]) + tuple(summed[k] for k in range(12))


def solution(mesh):
    return jax.shard_map(
        functools.partial(per_device, mesh.shape["inner"], mesh.shape["outer"]),
        mesh=mesh,
        in_specs=(
            P(("inner", "outer"), None, None, None),
            P(("inner", "outer")),
            P("inner"),
            P("inner"),
            P("inner", None),
            P("inner"),
            P("inner", None),
            P("inner"),
            P("inner"),
            P("inner"),
            P("inner", None),
            P("inner"),
            P("inner", None),
            P("inner"),
            P(("inner", "outer"), None, None, None),
        ),
        out_specs=(
            P(("inner", "outer"), None, None, None),
            P(("inner", "outer"), None, None, None),
            P("inner"),
            P("inner"),
            P("inner", None),
            P("inner"),
            P("inner", None),
            P("inner"),
            P("inner"),
            P("inner"),
            P("inner", None),
            P("inner"),
            P("inner", None),
            P("inner"),
        ),
        check_vma=False,
    )
```

time: 1290 us -> 852 us (0.66)
  waiting for transfers between devices: 645 us -> 235 us
  blocking collectives: 123 us -> 0 us
  starting transfers between devices: 2.52 us -> 102 us
  other arithmetic: 41.1 us -> 107 us
  matrix products: 297 us -> 260 us
  local copies, waits for them, and re-layouts: 158 us -> 139 us
  between operations: 20.8 us -> 3.39 us
    psum x1 -> x0, waiting for transfers between devices: 642 us -> none  [per_device(): lax.psum((totals[0], totals[1], totals[2], totals[3], totals[4], totals[5...]
    ppermute x0 -> x78, waiting for transfers between devices: none -> 235 us  [swap(): return lax.ppermute(tensor, axis, [(i, i ^ stride) for i in range(size)])]
    ppermute x0 -> x78, starting transfers between devices: none -> 102 us  [swap(): return lax.ppermute(tensor, axis, [(i, i ^ stride) for i in range(size)])]
    psum x1 -> x0, blocking collectives: 81.8 us -> none  [per_device(): lax.psum((totals[0], totals[1], totals[2], totals[3], totals[4], totals[5...]
    unnamed x293 -> x124, local copies, waits for them, and re-layouts: 79.3 us -> 14.5 us
    dot_general x8 -> x4, matrix products: 110 us -> 57.3 us  [outer_sum(): lax.dot_general(left, right, (((0,), (0,)), ((), ())), preferred_element_...]
    unnamed x3 -> x0, blocking collectives: 39.5 us -> none
    add x8 -> x33, other arithmetic: 0.04 us -> 32.5 us  [the longest x4 27 us: sum_to_owner(): mine = cut(grad, bit, rows) + arrived.astype(jnp.float32)]
  transfers between devices with their start and end apart: 9 -> 78, of which waited for: 2 -> 35; matrix products, arithmetic and copies ran while one was open for 30% -> 34% of each run, Pallas kernels for 0% -> 0%
where the time goes in v1:
time: 852 us; the launch traced here: 847 us
  matrix products  260 us (31%)
  waiting for transfers between devices  235 us (28%)
  local copies, waits for them, and re-layouts  139 us (16%)
  other arithmetic  107 us (13%)
  starting transfers between devices  102 us (12%)
    ppermute x78, waiting for transfers between devices, swap(): return lax.ppermute(tensor, axis, [(i, i ^ stride) for i in range(size)])  235 us
    ppermute x78, starting transfers between devices, swap(): return lax.ppermute(tensor, axis, [(i, i ^ stride) for i in range(size)])  102 us
    dot_general x4, matrix products, times_rows(): lax.dot_general(left, right, (((1,), (1,)), ((), ())), preferred_element_...  82.4 us
    dot_general x4, matrix products, matmul(): return jnp.dot(left, right, preferred_element_type=jnp.float32)  72.5 us
    reshape x8, local copies, waits for them, and re-layouts, split_heads(): return tensor.reshape(slot_count, length, HEADS, HEAD_DIM)  61.9 us
    dot_general x4, matrix products, outer_sum(): lax.dot_general(left, right, (((0,), (0,)), ((), ())), preferred_element_...  57.3 us
    add x4, other arithmetic, sum_to_owner(): mine = cut(grad, bit, rows) + arrived.astype(jnp.float32)  27 us
    convert_element_type x4, local copies, waits for them, and re-layouts, sum_to_owner(): arrived = swap(cut(grad, 1 - bit, rows).astype(jnp.bfloat16), 'inner', 2, 1)  22.1 us
  transfers between devices with their start and end apart: 78, of which 35 were waited for; matrix products, arithmetic and copies ran while one was open for 34% of the time, Pallas kernels for 0%

profile of v1, /device:TPU:0, one launch (start us, length us, event | category | flops | bytes accessed | tf_op | source)
XLA Modules:
  0.0 846.8 jit_solution(13647813143917748166)
XLA Ops:
  0.7 5.7 concatenate.367
  19.0 17.1 %fusion.52 = f32[1024,3456]{1,0:T(8,128)} fusion(bf16[1024,1152]{1,0:T(8,128)(2,1)S(1)} %fusion.26, bf16[576,3456]{1,0:T(8,128)(2,1)} %collective-permute-done.1, bf16[576,3456]{1,0:T(8,128)(2,1)} %param.19, pred[]{:T(512)S(6)} %eq.119), kind=kOutput, calls=%fused_computation.126 | convolution fusion | flops 8189558784 | bytes 24477696 | tf_op jit(solution)/shard_map/dot_general | solution.py:45
  36.1 4.0 slice.212
  40.1 5.9 fusion.16
  46.0 9.6 %reshape.378 = bf16[4,256,16,72]{3,2,1,0:T(8,128)(2,1)} reshape(bf16[1024,1152]{1,0:T(8,128)(2,1)} %get-tuple-element.73) | data formatting | bytes 4718592 | tf_op jit(solution)/shard_map/reshape | solution.py:204
  55.6 7.1 copy.121
  62.7 8.3 reshape.379
  71.0 5.7 copy.119
  76.7 9.9 %reshape.380 = bf16[4,256,16,72]{3,2,1,0:T(8,128)(2,1)} reshape(bf16[1024,1152]{1,0:T(8,128)(2,1)} %slice.212) | data formatting | bytes 4718592 | tf_op jit(solution)/shard_map/reshape | solution.py:204
  86.6 7.2 copy.120
  93.9 9.8 %multiply_reduce_fusion.1 = (f32[4,16,256]{2,1,0:T(8,128)S(1)}, f32[4,16,256,256]{2,3,1,0:T(8,128)}) fusion(bf16[4,256,16,72]{1,3,2,0:T(8,128)(2,1)S(1)} %copy.119, bf16[4,256,16,72]{1,3,2,0:T(8,128)(2,1)} %copy.120), kind=kOutput, calls=%fused_computation.17 | convolution fusion | flops 612352000 | bytes 21561344 | tf_op jit(solution)/shard_map/sqhd,skhd->shqk/dot_general | solution.py:240
  103.7 9.4 %fusion.7 = f32[4,16,256]{2,1,0:T(8,128)S(1)} fusion(f32[4,16,256,256]{2,3,1,0:T(8,128)} %get-tuple-element.85, f32[4,16,256]{2,1,0:T(8,128)S(1)} %get-tuple-element.84), kind=kLoop, calls=%fused_computation.16 | loop fusion | flops 12566528 | bytes 16908288 | tf_op jit(solution)/shard_map/reduce_sum | solution.py:247
  113.1 7.9 convert_bitcast_fusion.1
  123.5 6.7 fusion.105
  133.1 27.5 %multiply_convert_fusion = (bf16[1024,4304]{0,1:T(8,128)(2,1)}, f32[1024,4304]{0,1:T(8,128)}) fusion(f32[4304]{0:T(1024)S(1)} %fusion.80, bf16[576,4304]{1,0:T(8,128)(2,1)} %collective-permute-done.3, bf16[576,4304]{1,0:T(8,128)(2,1)} %param.25, pred[]{:T(512)S(6)} %eq.119, f32[1024,1152]{1,0:T(8,128)} %copy-done.8, f32[1152]{0:T(1024)S(1)} %fusion.86, ...), kind=kOutput, calls=%fused_computation.10 | convolution fusion | flops 10249005056 | bytes 41113408 | tf_op jit(solution)/shard_map/dot_general | solution.py:45
  160.6 31.8 %convert_reduce_fusion = (f32[4304]{0:T(1024)}, bf16[1024,4304]{0,1:T(8,128)(2,1)}) fusion(f32[1024,4304]{0,1:T(8,128)} %get-tuple-element.89, f32[4304]{0:T(1024)S(1)} %fusion.80, bf16[1024,1152]{1,0:T(8,128)(2,1)S(1)} %copy-done.21, bf16[2152,1152]{1,0:T(8,128)(2,1)} %collective-permute-done.4, bf16[2152,1152]{1,0:T(8,128)(2,1)} %param.27, pred[]{:T(512)S(6)} %eq.119), kind=kOutput, calls=%fused_computation.9 | convolution fusion | flops 10295990272 | bytes 38753920 | tf_op jit(solution)/shard_map/dot_general | solution.py:55
  192.4 24.5 %multiply_reduce_fusion.3 = (f32[1152]{0:T(1024)S(1)}, f32[1024]{0:T(1024)S(1)}, f32[1024]{0:T(1024)S(1)}, f32[1152]{0:T(1024)S(1)}, f32[1024,1152]{1,0:T(8,128)}) fusion(f32[1024,1152]{1,0:T(8,128)} %copy-done.8, f32[1024]{0:T(1024)S(1)} %add_rsqrt_fusion, f32[1024]{0:T(1024)S(1)} %broadcast_multiply_fusion.4, f32[1152]{0:T(1024)S(1)} %fusion.85, ...), kind=kOutput, calls=%fused_computation.66 | convolution fusion | flops 10209646592 | bytes 28198400 | tf_op jit(solution)/shard_map/dot_general | solution.py:55
  217.0 4.9 convert_reduce_fusion.2
  224.2 5.3 convolution_convert_fusion
  229.4 8.3 reshape.381
  237.8 5.7 copy.125
  243.5 12.7 %multiply_reduce_fusion = (f32[4,16,256]{2,1,0:T(8,128)S(1)}, f32[4,16,256,256]{2,3,1,0:T(8,128)}) fusion(f32[4,16,256,256]{2,3,1,0:T(8,128)} %get-tuple-element.85, f32[4,16,256]{2,1,0:T(8,128)S(1)} %log_add_fusion, bf16[4,256,16,72]{1,3,2,0:T(8,128)(2,1)S(1)} %copy.125, bf16[4,256,16,72]{1,3,2,0:T(8,128)(2,1)} %copy.121), kind=kOutput, calls=%fused_computation.12 | convolution fusion | flops 620740608 | bytes 38404096 | tf_op jit(solution)/shard_map/sqhd,skhd->shqk/dot_general | solution.py:298
  256.2 12.1 %multiply_convert_fusion.1 = bf16[4,16,256,256]{2,3,1,0:T(8,128)(2,1)S(1)} fusion(f32[4,16,256,256]{2,3,1,0:T(8,128)} %get-tuple-element.92, f32[4,16,256,256]{2,3,1,0:T(8,128)} %get-tuple-element.85, f32[4,16,256]{2,1,0:T(8,128)S(1)} %get-tuple-element.91, f32[4,16,256]{2,1,0:T(8,128)S(1)} %log_add_fusion), kind=kLoop, calls=%fused_computation.11 | loop fusion | flops 20971520 | bytes 42074112 | tf_op jit(solution)/shard_map/convert_element_type | solution.py:302
  271.5 4.1 fusion.40
  275.6 10.6 %convert_reduce_fusion.3 = (f32[16,72]{1,0:T(8,128)S(1)}, bf16[4,256,16,72]{1,3,2,0:T(8,128)(2,1)}) fusion(bf16[4,256,16,72]{1,3,2,0:T(8,128)(2,1)S(1)} %copy.125, f32[4,16,256,256]{2,3,1,0:T(8,128)} %get-tuple-element.85, f32[4,16,256]{2,1,0:T(8,128)S(1)} %log_add_fusion), kind=kOutput, calls=%fused_computation.68 | convolution fusion | flops 620100480 | bytes 21565952 | tf_op jit(solution)/shard_map/shqk,sqhd->skhd/dot_general | solution.py:292
  286.1 8.6 %fusion.96 = f32[1152,1152]{1,0:T(8,128)} fusion(bf16[1024,1152]{0,1:T(8,128)(2,1)} %bitcast.121, f32[1024,1152]{1,0:T(8,128)} %copy-done.9), kind=kOutput, calls=%fused_computation.281 | convolution fusion | flops 2719088640 | bytes 12386304 | tf_op jit(solution)/shard_map/dot_general | solution.py:49
  294.8 18.6 %fusion.102 = f32[1152,4304]{1,0:T(8,128)} fusion(bf16[1024,4304]{0,1:T(8,128)(2,1)} %get-tuple-element.99, f32[1024,1152]{1,0:T(8,128)S(1)} %bitcast.102, f32[1152]{0:T(1024)S(1)} %fusion.86, f32[1152]{0:T(1024)S(1)} %fusion.85, f32[1024]{0:T(1024)S(1)} %add_rsqrt_fusion, f32[1024]{0:T(1024)S(1)} %broadcast_multiply_fusion.4), kind=kOutput, calls=%fused_computation.287 | convolution fusion | flops 10160308224 | bytes 33383424 | tf_op jit(solution)/shard_map/dot_general | solution.py:49
  325.1 12.0 %fusion.106 = f32[1152,3456]{1,0:T(8,128)} fusion(bf16[1024,1152]{1,0:T(8,128)(2,1)S(1)} %copy-done.19, bf16[1024,3456]{0,1:T(8,128)(2,1)S(1)} %constant_dynamic-update-slice_fusion), kind=kOutput, calls=%fused_computation.291 | convolution fusion | flops 8153726976 | bytes 25362432 | tf_op jit(solution)/shard_map/dot_general | solution.py:49
  337.2 20.8 %fusion.32 = (f32[1152]{0:T(1024)S(1)}, f32[1024]{0:T(1024)S(1)}, f32[1024]{0:T(1024)S(1)}, f32[1152]{0:T(1024)S(1)}, f32[1024,1152]{1,0:T(8,128)}) fusion(bf16[1,4,256,1152]{3,2,1,0:T(8,128)(2,1)S(1)} %copy-done.4, f32[1024]{0:T(1024)S(1)} %bitcast.127, f32[1024]{0:T(1024)S(1)} %bitcast.130, f32[1152]{0:T(1024)S(1)} %copy-done.25, ...), kind=kOutput, calls=%fused_computation.63 | convolution fusion | flops 8201351168 | bytes 22148608 | tf_op jit(solution)/shard_map/dot_general | solution.py:55
  358.4 5.6 dynamic-slice_convert_fusion.2
  367.6 6.8 dynamic-slice_convert_fusion
  374.9 21.3 %fusion.35 = bf16[1024,1152]{1,0:T(8,128)(2,1)} fusion(f32[1024,1152]{1,0:T(8,128)S(1)} %bitcast.104, bf16[1024,4304]{0,1:T(8,128)(2,1)} %get-tuple-element.88, f32[1024]{0:T(1024)S(1)} %bitcast.125, f32[1152]{0:T(1024)S(1)} %copy-done.42, bf16[2152,1152]{1,0:T(8,128)(2,1)} %collective-permute-done.4, bf16[2152,1152]{1,0:T(8,128)(2,1)} %param.27, pred[]{:T(512)S(6)} %eq.119), kind=kOutput, calls=%fused_computation.83 | convolution fusion | flops 10203752448 | bytes 25817600 | tf_op jit(solution)/shard_map/dot_general | solution.py:45
  398.9 18.0 %fusion.107 = f32[4304,1152]{1,0:T(8,128)} fusion(bf16[1024,4304]{0,1:T(8,128)(2,1)} %get-tuple-element.88, bf16[1024,1152]{1,0:T(8,128)(2,1)S(1)} %copy-done.22), kind=kOutput, calls=%fused_computation.292 | convolution fusion | flops 10154409984 | bytes 31006720 | tf_op jit(solution)/shard_map/dot_general | solution.py:49
  435.0 4.6 collective-permute-done.29
  466.1 6.6 dynamic-slice_convert_fusion.1
  475.4 5.1 convert_add_fusion.2
  492.8 11.3 %collective-permute-done.11 = bf16[288,1664]{1,0:T(8,128)(2,1)S(1)} collective-permute-done((bf16[288,1664]{1,0:T(8,128)(2,1)S(1)}, bf16[288,1664]{1,0:T(8,128)(2,1)S(1)}, u32[]{:S(2)}, u32[]{:S(2)}) %collective-permute-start.11) | collective-permute-done | bytes 958496 | tf_op jit(solution)/shard_map/ppermute | solution.py:65
  508.0 10.2 %convert_add_fusion = f32[576,4304]{1,0:T(8,128)} fusion(bf16[576,4304]{1,0:T(8,128)(2,1)} %collective-permute-done.44, f32[1152,4304]{1,0:T(8,128)} %fusion.102, s32[]{:T(128)S(6)} %select_n.727), kind=kLoop, calls=%fused_computation.20 | loop fusion | flops 4958208 | bytes 24791044 | tf_op jit(solution)/shard_map/add | solution.py:116
  521.1 5.1 slice.191
  526.2 10.0 %convert_add_fusion.1 = f32[2152,1152]{1,0:T(8,128)} fusion(bf16[2152,1152]{1,0:T(8,128)(2,1)} %collective-permute-done.61, f32[4304,1152]{1,0:T(8,128)} %fusion.107, s32[]{:T(128)S(6)} %select_n.797), kind=kLoop, calls=%fused_computation.23 | loop fusion | flops 4958208 | bytes 24791044 | tf_op jit(solution)/shard_map/add | solution.py:116
  550.1 54.1 %collective-permute-done.20 = bf16[144,1792]{1,0:T(8,128)(2,1)S(1)} collective-permute-done((bf16[144,1792]{1,0:T(8,128)(2,1)S(1)}, bf16[144,1792]{1,0:T(8,128)(2,1)S(1)}, u32[]{:S(2)}, u32[]{:S(2)}) %collective-permute-start.20) | collective-permute-done | bytes 516128 | tf_op jit(solution)/shard_map/ppermute | solution.py:65
  606.3 4.5 collective-permute-done.13
  613.2 5.6 collective-permute-done.21
  621.9 6.4 collective-permute-done.14
  628.5 8.8 %collective-permute-done.15 = bf16[40,1664]{1,0:T(8,128)(2,1)S(1)} collective-permute-done((bf16[40,1664]{1,0:T(8,128)(2,1)S(1)}, bf16[40,1664]{1,0:T(8,128)(2,1)S(1)}, u32[]{:S(2)}, u32[]{:S(2)}) %collective-permute-start.15) | collective-permute-done | bytes 133152 | tf_op jit(solution)/shard_map/ppermute | solution.py:65
  637.3 8.3 collective-permute-done.22
  648.6 5.0 collective-permute-done.23
  664.4 4.2 collective-permute-done.63
  668.8 13.0 %collective-permute-done.17 = bf16[144,1664]{1,0:T(8,128)(2,1)S(1)} collective-permute-done((bf16[144,1664]{1,0:T(8,128)(2,1)S(1)}, bf16[144,1664]{1,0:T(8,128)(2,1)S(1)}, u32[]{:S(2)}, u32[]{:S(2)}) %collective-permute-start.17) | collective-permute-done | bytes 479264 | tf_op jit(solution)/shard_map/ppermute | solution.py:65
  681.9 3.8 collective-permute-start.64
  686.3 4.4 collective-permute-done.25
  708.1 6.2 collective-permute-done.66
  714.2 3.9 collective-permute-start.72
  720.2 14.7 %collective-permute-done.49 = bf16[40,2048]{1,0:T(8,128)(2,1)S(1)} collective-permute-done((bf16[40,2048]{1,0:T(8,128)(2,1)S(1)}, bf16[40,2048]{1,0:T(8,128)(2,1)S(1)}, u32[]{:S(2)}, u32[]{:S(2)}) %collective-permute-start.49) | collective-permute-done | bytes 163872 | tf_op jit(solution)/shard_map/ppermute | solution.py:65
  738.6 7.4 collective-permute-done.56
  763.1 3.7 collective-permute-start.75
  772.4 7.5 collective-permute-done.51
  780.4 5.3 collective-permute-done.59
  787.1 3.8 maximum_convert_fusion.2
  790.9 26.2 %collective-permute-done.76 = bf16[544,640]{1,0:T(8,128)(2,1)S(1)} collective-permute-done((bf16[544,640]{1,0:T(8,128)(2,1)S(1)}, bf16[544,640]{1,0:T(8,128)(2,1)S(1)}, u32[]{:S(2)}, u32[]{:S(2)}) %collective-permute-start.76) | collective-permute-done | bytes 696352 | tf_op jit(solution)/shard_map/ppermute | solution.py:65
  818.6 11.2 %collective-permute-done.52 = bf16[288,2048]{1,0:T(8,128)(2,1)S(1)} collective-permute-done((bf16[288,2048]{1,0:T(8,128)(2,1)S(1)}, bf16[288,2048]{1,0:T(8,128)(2,1)S(1)}, u32[]{:S(2)}, u32[]{:S(2)}) %collective-permute-start.52) | collective-permute-done | bytes 1179680 | tf_op jit(solution)/shard_map/ppermute | solution.py:65
  832.2 4.7 maximum_convert_fusion
  837.0 5.0 fusion.38
  842.0 4.5 maximum_convert_fusion.1
  (426 shorter events, 194.5 us)
Async XLA Ops:
  6.4 10.2 %collective-permute-start = (bf16[1,6760]{1,0:T(2,128)(2,1)S(1)}, bf16[1,6760]{1,0:T(2,128)(2,1)S(1)}, u32[]{:S(2)}, u32[]{:S(2)}) collective-permute-start(bf16[1,6760]{1,0:T(2,128)(2,1)S(1)} %reshape.366), channel_id=1, source_target_pairs={{0,16},{16,0},{1,17},{17,1},{2,18},{18,2},{3,19},{19,3},{4,20},{20... | collective-permute-start | bytes 40568 | tf_op jit(solution)/shard_map/ppermute | solution.py:65
  7.0 12.0 %collective-permute-start.1 = (bf16[576,3456]{1,0:T(8,128)(2,1)}, bf16[576,3456]{1,0:T(8,128)(2,1)}, u32[]{:S(2)}, u32[]{:S(2)}) collective-permute-start(bf16[576,3456]{1,0:T(8,128)(2,1)} %param.19), channel_id=1, source_target_pairs={{0,16},{16,0},{1,17},{17,1},{2,18},{18,2},{3,19},{19,3},{4,20},{20... | collective-permute-start | bytes 11943944 | tf_op jit(solution)/shard_map/ppermute | solution.py:65
  7.0 116.4 %collective-permute-start.2 = (bf16[576,1152]{1,0:T(8,128)(2,1)}, bf16[576,1152]{1,0:T(8,128)(2,1)}, u32[]{:S(2)}, u32[]{:S(2)}) collective-permute-start(bf16[576,1152]{1,0:T(8,128)(2,1)} %param.21), channel_id=1, source_target_pairs={{0,16},{16,0},{1,17},{17,1},{2,18},{18,2},{3,19},{19,3},{4,20},{20... | collective-permute-start | bytes 3981320 | tf_op jit(solution)/shard_map/ppermute | solution.py:65
  7.5 125.6 %collective-permute-start.3 = (bf16[576,4304]{1,0:T(8,128)(2,1)}, bf16[576,4304]{1,0:T(8,128)(2,1)}, u32[]{:S(2)}, u32[]{:S(2)}) collective-permute-start(bf16[576,4304]{1,0:T(8,128)(2,1)} %param.25), channel_id=1, source_target_pairs={{0,16},{16,0},{1,17},{17,1},{2,18},{18,2},{3,19},{19,3},{4,20},{20... | collective-permute-start | bytes 14874632 | tf_op jit(solution)/shard_map/ppermute | solution.py:65
  7.6 153.0 %collective-permute-start.4 = (bf16[2152,1152]{1,0:T(8,128)(2,1)}, bf16[2152,1152]{1,0:T(8,128)(2,1)}, u32[]{:S(2)}, u32[]{:S(2)}) collective-permute-start(bf16[2152,1152]{1,0:T(8,128)(2,1)} %param.27), channel_id=1, source_target_pairs={{0,16},{16,0},{1,17},{17,1},{2,18},{18,2},{3,19},{19,3},{4,20},{20... | collective-permute-start | bytes 14874632 | tf_op jit(solution)/shard_map/ppermute | solution.py:65
  358.2 37.9 %collective-permute-start.5 = (f32[8,1792]{1,0:T(8,128)S(1)}, f32[8,1792]{1,0:T(8,128)S(1)}, u32[]{:S(2)}, u32[]{:S(2)}) collective-permute-start(f32[8,1792]{1,0:T(8,128)S(1)} %reshape.374), channel_id=1, source_target_pairs={{0,16},{16,0},{1,17},{17,1},{2,18},{18,2},{3,19},{19,3},{4,20},{20... | collective-permute-start | bytes 172040 | tf_op jit(solution)/shard_map/ppermute | solution.py:65
  364.0 111.4 %collective-permute-start.10 = (bf16[576,3456]{1,0:T(8,128)(2,1)}, bf16[576,3456]{1,0:T(8,128)(2,1)}, u32[]{:S(2)}, u32[]{:S(2)}) collective-permute-start(bf16[576,3456]{1,0:T(8,128)(2,1)} %dynamic-slice_convert_fusion.2), channel_id=1, source_target_pairs={{0,16},{16,0},{1,17},{17,1},{2,18},{18,2},{3,19},{19,3},{4,20},{20... | collective-permute-start | bytes 11943944 | tf_op jit(solution)/shard_map/ppermute | solution.py:65
  367.5 55.8 %collective-permute-start.27 = (bf16[576,1152]{1,0:T(8,128)(2,1)}, bf16[576,1152]{1,0:T(8,128)(2,1)}, u32[]{:S(2)}, u32[]{:S(2)}) collective-permute-start(bf16[576,1152]{1,0:T(8,128)(2,1)} %dynamic-slice_convert_fusion.4), channel_id=1, source_target_pairs={{0,16},{16,0},{1,17},{17,1},{2,18},{18,2},{3,19},{19,3},{4,20},{20... | collective-permute-start | bytes 3981320 | tf_op jit(solution)/shard_map/ppermute | solution.py:65
  374.4 133.5 %collective-permute-start.44 = (bf16[576,4304]{1,0:T(8,128)(2,1)}, bf16[576,4304]{1,0:T(8,128)(2,1)}, u32[]{:S(2)}, u32[]{:S(2)}) collective-permute-start(bf16[576,4304]{1,0:T(8,128)(2,1)} %dynamic-slice_convert_fusion), channel_id=1, source_target_pairs={{0,16},{16,0},{1,17},{17,1},{2,18},{18,2},{3,19},{19,3},{4,20},{20... | collective-permute-start | bytes 14874632 | tf_op jit(solution)/shard_map/ppermute | solution.py:65
  396.2 20.7 %collective-permute-start.6 = (f32[8,1792]{1,0:T(8,128)S(1)}, f32[8,1792]{1,0:T(8,128)S(1)}, u32[]{:S(2)}, u32[]{:S(2)}) collective-permute-start(f32[8,1792]{1,0:T(8,128)S(1)} %add.491), channel_id=1, source_target_pairs={{0,1},{1,0},{2,3},{3,2},{4,5},{5,4},{6,7},{7,6},{8,9},{9,8},{10,11... | collective-permute-start | bytes 172040 | tf_op jit(solution)/shard_map/ppermute | solution.py:65
  421.2 9.1 %collective-permute-start.8 = (f32[8,1792]{1,0:T(8,128)S(1)}, f32[8,1792]{1,0:T(8,128)S(1)}, u32[]{:S(2)}, u32[]{:S(2)}) collective-permute-start(f32[8,1792]{1,0:T(8,128)S(1)} %add.493), channel_id=1, source_target_pairs={{0,4},{1,5},{2,6},{3,7},{4,0},{5,1},{6,2},{7,3},{8,12},{9,13},{10,... | collective-permute-start | bytes 172040 | tf_op jit(solution)/shard_map/ppermute | solution.py:65
  425.3 9.6 %collective-permute-start.36 = (bf16[288,640]{1,0:T(8,128)(2,1)S(1)}, bf16[288,640]{1,0:T(8,128)(2,1)S(1)}, u32[]{:S(2)}, u32[]{:S(2)}) collective-permute-start(bf16[288,640]{1,0:T(8,128)(2,1)S(1)} %dynamic-slice_convert_fusion.12), channel_id=1, source_target_pairs={{0,2},{1,3},{2,0},{3,1},{4,6},{5,7},{6,4},{7,5},{8,10},{9,11},{10,... | collective-permute-start | bytes 1105928 | tf_op jit(solution)/shard_map/ppermute | solution.py:65
  427.0 7.2 collective-permute-start.28
  430.3 42.4 %collective-permute-start.9 = (f32[8,1792]{1,0:T(8,128)S(1)}, f32[8,1792]{1,0:T(8,128)S(1)}, u32[]{:S(2)}, u32[]{:S(2)}) collective-permute-start(f32[8,1792]{1,0:T(8,128)S(1)} %add.494), channel_id=1, source_target_pairs={{0,8},{1,9},{2,10},{3,11},{4,12},{5,13},{6,14},{7,15},{8,0},{9,1},... | collective-permute-start | bytes 172040 | tf_op jit(solution)/shard_map/ppermute | solution.py:65
  463.7 9.1 %collective-permute-start.34 = (bf16[144,512]{1,0:T(8,128)(2,1)S(1)}, bf16[144,512]{1,0:T(8,128)(2,1)S(1)}, u32[]{:S(2)}, u32[]{:S(2)}) collective-permute-start(bf16[144,512]{1,0:T(8,128)(2,1)S(1)} %maximum_select_fusion.33), channel_id=1, source_target_pairs={{0,2},{1,3},{2,0},{3,1},{4,6},{5,7},{6,4},{7,5},{8,10},{9,11},{10,... | collective-permute-start | bytes 442376 | tf_op jit(solution)/shard_map/ppermute | solution.py:65
  466.0 8.9 %collective-permute-start.42 = (bf16[144,640]{1,0:T(8,128)(2,1)S(1)}, bf16[144,640]{1,0:T(8,128)(2,1)S(1)}, u32[]{:S(2)}, u32[]{:S(2)}) collective-permute-start(bf16[144,640]{1,0:T(8,128)(2,1)S(1)} %maximum_select_fusion.32), channel_id=1, source_target_pairs={{0,1},{1,0},{2,3},{3,2},{4,5},{5,4},{6,7},{7,6},{8,9},{9,8},{10,11... | collective-permute-start | bytes 552968 | tf_op jit(solution)/shard_map/ppermute | solution.py:65
  472.7 53.5 %collective-permute-start.61 = (bf16[2152,1152]{1,0:T(8,128)(2,1)}, bf16[2152,1152]{1,0:T(8,128)(2,1)}, u32[]{:S(2)}, u32[]{:S(2)}) collective-permute-start(bf16[2152,1152]{1,0:T(8,128)(2,1)} %dynamic-slice_convert_fusion.1), channel_id=1, source_target_pairs={{0,16},{16,0},{1,17},{17,1},{2,18},{18,2},{3,19},{19,3},{4,20},{20... | collective-permute-start | bytes 14874632 | tf_op jit(solution)/shard_map/ppermute | solution.py:65
  472.8 14.1 %collective-permute-start.35 = (bf16[288,512]{1,0:T(8,128)(2,1)S(1)}, bf16[288,512]{1,0:T(8,128)(2,1)S(1)}, u32[]{:S(2)}, u32[]{:S(2)}) collective-permute-start(bf16[288,512]{1,0:T(8,128)(2,1)S(1)} %maximum_select_fusion.30), channel_id=1, source_target_pairs={{0,1},{1,0},{2,3},{3,2},{4,5},{5,4},{6,7},{7,6},{8,9},{9,8},{10,11... | collective-permute-start | bytes 884744 | tf_op jit(solution)/shard_map/ppermute | solution.py:65
  474.9 12.2 %collective-permute-start.43 = (bf16[288,640]{1,0:T(8,128)(2,1)S(1)}, bf16[288,640]{1,0:T(8,128)(2,1)S(1)}, u32[]{:S(2)}, u32[]{:S(2)}) collective-permute-start(bf16[288,640]{1,0:T(8,128)(2,1)S(1)} %maximum_select_fusion.28), channel_id=1, source_target_pairs={{0,2},{1,3},{2,0},{3,1},{4,6},{5,7},{6,4},{7,5},{8,10},{9,11},{10,... | collective-permute-start | bytes 1105928 | tf_op jit(solution)/shard_map/ppermute | solution.py:65
  480.9 23.1 %collective-permute-start.11 = (bf16[288,1664]{1,0:T(8,128)(2,1)S(1)}, bf16[288,1664]{1,0:T(8,128)(2,1)S(1)}, u32[]{:S(2)}, u32[]{:S(2)}) collective-permute-start(bf16[288,1664]{1,0:T(8,128)(2,1)S(1)} %dynamic-slice_convert_fusion.7), channel_id=1, source_target_pairs={{0,1},{1,0},{2,3},{3,2},{4,5},{5,4},{6,7},{7,6},{8,9},{9,8},{10,11... | collective-permute-start | bytes 2875400 | tf_op jit(solution)/shard_map/ppermute | solution.py:65
  491.5 53.7 %collective-permute-start.19 = (bf16[288,1792]{1,0:T(8,128)(2,1)S(1)}, bf16[288,1792]{1,0:T(8,128)(2,1)}, u32[]{:S(2)}, u32[]{:S(2)}) collective-permute-start(bf16[288,1792]{1,0:T(8,128)(2,1)S(1)} %dynamic-slice_convert_fusion.6), channel_id=1, source_target_pairs={{0,2},{1,3},{2,0},{3,1},{4,6},{5,7},{6,4},{7,5},{8,10},{9,11},{10,... | collective-permute-start | bytes 3096584 | tf_op jit(solution)/shard_map/ppermute | solution.py:65
  506.4 42.1 %collective-permute-start.12 = (bf16[144,1664]{1,0:T(8,128)(2,1)}, bf16[144,1664]{1,0:T(8,128)(2,1)}, u32[]{:S(2)}, u32[]{:S(2)}) collective-permute-start(bf16[144,1664]{1,0:T(8,128)(2,1)} %dynamic-slice_convert_fusion.11), channel_id=1, source_target_pairs={{0,2},{1,3},{2,0},{3,1},{4,6},{5,7},{6,4},{7,5},{8,10},{9,11},{10,... | collective-permute-start | bytes 1437704 | tf_op jit(solution)/shard_map/ppermute | solution.py:65
  542.2 117.1 %collective-permute-start.53 = (bf16[288,2256]{1,0:T(8,128)(2,1)S(1)}, bf16[288,2256]{1,0:T(8,128)(2,1)S(1)}, u32[]{:S(2)}, u32[]{:S(2)}) collective-permute-start(bf16[288,2256]{1,0:T(8,128)(2,1)S(1)} %dynamic-slice_convert_fusion.3), channel_id=1, source_target_pairs={{0,2},{1,3},{2,0},{3,1},{4,6},{5,7},{6,4},{7,5},{8,10},{9,11},{10,... | collective-permute-start | bytes 3898376 | tf_op jit(solution)/shard_map/ppermute | solution.py:65
  542.9 111.5 %collective-permute-start.45 = (bf16[288,2048]{1,0:T(8,128)(2,1)S(1)}, bf16[288,2048]{1,0:T(8,128)(2,1)S(1)}, u32[]{:S(2)}, u32[]{:S(2)}) collective-permute-start(bf16[288,2048]{1,0:T(8,128)(2,1)S(1)} %dynamic-slice_convert_fusion.5), channel_id=1, source_target_pairs={{0,1},{1,0},{2,3},{3,2},{4,5},{5,4},{6,7},{7,6},{8,9},{9,8},{10,11... | collective-permute-start | bytes 3538952 | tf_op jit(solution)/shard_map/ppermute | solution.py:65
  543.8 118.1 %collective-permute-start.70 = (bf16[1080,640]{1,0:T(8,128)(2,1)S(1)}, bf16[1080,640]{1,0:T(8,128)(2,1)S(1)}, u32[]{:S(2)}, u32[]{:S(2)}) collective-permute-start(bf16[1080,640]{1,0:T(8,128)(2,1)S(1)} %fusion.37), channel_id=1, source_target_pairs={{0,2},{1,3},{2,0},{3,1},{4,6},{5,7},{6,4},{7,5},{8,10},{9,11},{10,... | collective-permute-start | bytes 4147208 | tf_op jit(solution)/shard_map/ppermute | solution.py:65
  545.2 100.4 %collective-permute-start.62 = (bf16[1080,512]{1,0:T(8,128)(2,1)S(1)}, bf16[1080,512]{1,0:T(8,128)(2,1)S(1)}, u32[]{:S(2)}, u32[]{:S(2)}) collective-permute-start(bf16[1080,512]{1,0:T(8,128)(2,1)S(1)} %fusion.42), channel_id=1, source_target_pairs={{0,1},{1,0},{2,3},{3,2},{4,5},{5,4},{6,7},{7,6},{8,9},{9,8},{10,11... | collective-permute-start | bytes 3317768 | tf_op jit(solution)/shard_map/ppermute | solution.py:65
  548.5 55.7 %collective-permute-start.20 = (bf16[144,1792]{1,0:T(8,128)(2,1)S(1)}, bf16[144,1792]{1,0:T(8,128)(2,1)S(1)}, u32[]{:S(2)}, u32[]{:S(2)}) collective-permute-start(bf16[144,1792]{1,0:T(8,128)(2,1)S(1)} %dynamic-slice_convert_fusion.10), channel_id=1, source_target_pairs={{0,1},{1,0},{2,3},{3,2},{4,5},{5,4},{6,7},{7,6},{8,9},{9,8},{10,11... | collective-permute-start | bytes 1548296 | tf_op jit(solution)/shard_map/ppermute | solution.py:65
  610.8 8.0 collective-permute-start.21
  618.8 9.5 %collective-permute-start.14 = (bf16[40,1664]{1,0:T(8,128)(2,1)S(1)}, bf16[40,1664]{1,0:T(8,128)(2,1)S(1)}, u32[]{:S(2)}, u32[]{:S(2)}) collective-permute-start(bf16[40,1664]{1,0:T(8,128)(2,1)S(1)} %fusion.69), channel_id=1, source_target_pairs={{0,8},{1,9},{2,10},{3,11},{4,12},{5,13},{6,14},{7,15},{8,0},{9,1},... | collective-permute-start | bytes 399368 | tf_op jit(solution)/shard_map/ppermute | solution.py:65
  628.4 8.9 %collective-permute-start.15 = (bf16[40,1664]{1,0:T(8,128)(2,1)S(1)}, bf16[40,1664]{1,0:T(8,128)(2,1)S(1)}, u32[]{:S(2)}, u32[]{:S(2)}) collective-permute-start(bf16[40,1664]{1,0:T(8,128)(2,1)S(1)} %fusion.68), channel_id=1, source_target_pairs={{0,8},{1,9},{2,10},{3,11},{4,12},{5,13},{6,14},{7,15},{8,0},{9,1},... | collective-permute-start | bytes 399368 | tf_op jit(solution)/shard_map/ppermute | solution.py:65
  637.2 8.4 collective-permute-start.22
  645.6 12.5 %collective-permute-start.16 = (bf16[72,1664]{1,0:T(8,128)(2,1)S(1)}, bf16[72,1664]{1,0:T(8,128)(2,1)S(1)}, u32[]{:S(2)}, u32[]{:S(2)}) collective-permute-start(bf16[72,1664]{1,0:T(8,128)(2,1)S(1)} %fusion.71), channel_id=1, source_target_pairs={{0,4},{1,5},{2,6},{3,7},{4,0},{5,1},{6,2},{7,3},{8,12},{9,13},{10,... | collective-permute-start | bytes 718856 | tf_op jit(solution)/shard_map/ppermute | solution.py:65
  645.7 7.9 collective-permute-start.23
  653.6 15.0 %collective-permute-start.63 = (bf16[544,512]{1,0:T(8,128)(2,1)S(1)}, bf16[544,512]{1,0:T(8,128)(2,1)S(1)}, u32[]{:S(2)}, u32[]{:S(2)}) collective-permute-start(bf16[544,512]{1,0:T(8,128)(2,1)S(1)} %fusion.54), channel_id=1, source_target_pairs={{0,2},{1,3},{2,0},{3,1},{4,6},{5,7},{6,4},{7,5},{8,10},{9,11},{10,... | collective-permute-start | bytes 1671176 | tf_op jit(solution)/shard_map/ppermute | solution.py:65
  654.3 7.5 collective-permute-start.24
  658.1 27.8 %collective-permute-start.46 = (bf16[144,2048]{1,0:T(8,128)(2,1)S(1)}, bf16[144,2048]{1,0:T(8,128)(2,1)S(1)}, u32[]{:S(2)}, u32[]{:S(2)}) collective-permute-start(bf16[144,2048]{1,0:T(8,128)(2,1)S(1)} %dynamic-slice_convert_fusion.9), channel_id=1, source_target_pairs={{0,2},{1,3},{2,0},{3,1},{4,6},{5,7},{6,4},{7,5},{8,10},{9,11},{10,... | collective-permute-start | bytes 1769480 | tf_op jit(solution)/shard_map/ppermute | solution.py:65
  659.3 22.5 %collective-permute-start.17 = (bf16[144,1664]{1,0:T(8,128)(2,1)S(1)}, bf16[144,1664]{1,0:T(8,128)(2,1)S(1)}, u32[]{:S(2)}, u32[]{:S(2)}) collective-permute-start(bf16[144,1664]{1,0:T(8,128)(2,1)S(1)} %maximum_select_fusion.25), channel_id=1, source_target_pairs={{0,2},{1,3},{2,0},{3,1},{4,6},{5,7},{6,4},{7,5},{8,10},{9,11},{10,... | collective-permute-start | bytes 1437704 | tf_op jit(solution)/shard_map/ppermute | solution.py:65
  661.9 33.5 %collective-permute-start.54 = (bf16[144,2256]{1,0:T(8,128)(2,1)S(1)}, bf16[144,2256]{1,0:T(8,128)(2,1)S(1)}, u32[]{:S(2)}, u32[]{:S(2)}) collective-permute-start(bf16[144,2256]{1,0:T(8,128)(2,1)S(1)} %dynamic-slice_convert_fusion.8), channel_id=1, source_target_pairs={{0,1},{1,0},{2,3},{3,2},{4,5},{5,4},{6,7},{7,6},{8,9},{9,8},{10,11... | collective-permute-start | bytes 1949192 | tf_op jit(solution)/shard_map/ppermute | solution.py:65
  662.0 28.7 %collective-permute-start.25 = (bf16[144,1792]{1,0:T(8,128)(2,1)S(1)}, bf16[144,1792]{1,0:T(8,128)(2,1)S(1)}, u32[]{:S(2)}, u32[]{:S(2)}) collective-permute-start(bf16[144,1792]{1,0:T(8,128)(2,1)S(1)} %maximum_select_fusion.24), channel_id=1, source_target_pairs={{0,1},{1,0},{2,3},{3,2},{4,5},{5,4},{6,7},{7,6},{8,9},{9,8},{10,11... | collective-permute-start | bytes 1548296 | tf_op jit(solution)/shard_map/ppermute | solution.py:65
  668.6 37.0 %collective-permute-start.71 = (bf16[544,640]{1,0:T(8,128)(2,1)S(1)}, bf16[544,640]{1,0:T(8,128)(2,1)S(1)}, u32[]{:S(2)}, u32[]{:S(2)}) collective-permute-start(bf16[544,640]{1,0:T(8,128)(2,1)S(1)} %fusion.49), channel_id=1, source_target_pairs={{0,1},{1,0},{2,3},{3,2},{4,5},{5,4},{6,7},{7,6},{8,9},{9,8},{10,11... | collective-permute-start | bytes 2088968 | tf_op jit(solution)/shard_map/ppermute | solution.py:65
  681.9 13.1 %collective-permute-start.64 = (bf16[272,512]{1,0:T(8,128)(2,1)S(1)}, bf16[272,512]{1,0:T(8,128)(2,1)S(1)}, u32[]{:S(2)}, u32[]{:S(2)}) collective-permute-start(bf16[272,512]{1,0:T(8,128)(2,1)S(1)} %dynamic-slice_convert_fusion.17), channel_id=1, source_target_pairs={{0,4},{1,5},{2,6},{3,7},{4,0},{5,1},{6,2},{7,3},{8,12},{9,13},{10,... | collective-permute-start | bytes 835592 | tf_op jit(solution)/shard_map/ppermute | solution.py:65
  685.9 73.1 %collective-permute-start.18 = (bf16[288,1664]{1,0:T(8,128)(2,1)S(1)}, bf16[288,1664]{1,0:T(8,128)(2,1)S(1)}, u32[]{:S(2)}, u32[]{:S(2)}) collective-permute-start(bf16[288,1664]{1,0:T(8,128)(2,1)S(1)} %maximum_select_fusion.17), channel_id=1, source_target_pairs={{0,1},{1,0},{2,3},{3,2},{4,5},{5,4},{6,7},{7,6},{8,9},{9,8},{10,11... | collective-permute-start | bytes 2875400 | tf_op jit(solution)/shard_map/ppermute | solution.py:65
  690.7 7.7 collective-permute-start.47
  695.0 71.9 %collective-permute-start.26 = (bf16[288,1792]{1,0:T(8,128)(2,1)S(1)}, bf16[288,1792]{1,0:T(8,128)(2,1)S(1)}, u32[]{:S(2)}, u32[]{:S(2)}) collective-permute-start(bf16[288,1792]{1,0:T(8,128)(2,1)S(1)} %maximum_select_fusion.16), channel_id=1, source_target_pairs={{0,2},{1,3},{2,0},{3,1},{4,6},{5,7},{6,4},{7,5},{8,10},{9,11},{10,... | collective-permute-start | bytes 3096584 | tf_op jit(solution)/shard_map/ppermute | solution.py:65
  695.4 6.9 collective-permute-start.65
  698.4 20.0 %collective-permute-start.55 = (bf16[72,2256]{1,0:T(8,128)(2,1)S(1)}, bf16[72,2256]{1,0:T(8,128)(2,1)S(1)}, u32[]{:S(2)}, u32[]{:S(2)}) collective-permute-start(bf16[72,2256]{1,0:T(8,128)(2,1)S(1)} %dynamic-slice_convert_fusion.14), channel_id=1, source_target_pairs={{0,4},{1,5},{2,6},{3,7},{4,0},{5,1},{6,2},{7,3},{8,12},{9,13},{10,... | collective-permute-start | bytes 974600 | tf_op jit(solution)/shard_map/ppermute | solution.py:65
  702.3 15.9 %collective-permute-start.48 = (bf16[40,2048]{1,0:T(8,128)(2,1)S(1)}, bf16[40,2048]{1,0:T(8,128)(2,1)S(1)}, u32[]{:S(2)}, u32[]{:S(2)}) collective-permute-start(bf16[40,2048]{1,0:T(8,128)(2,1)S(1)} %fusion.62), channel_id=1, source_target_pairs={{0,8},{1,9},{2,10},{3,11},{4,12},{5,13},{6,14},{7,15},{8,0},{9,1},... | collective-permute-start | bytes 491528 | tf_op jit(solution)/shard_map/ppermute | solution.py:65
  705.6 8.6 %collective-permute-start.66 = (bf16[136,512]{1,0:T(8,128)(2,1)S(1)}, bf16[136,512]{1,0:T(8,128)(2,1)S(1)}, u32[]{:S(2)}, u32[]{:S(2)}) collective-permute-start(bf16[136,512]{1,0:T(8,128)(2,1)S(1)} %add_convert_fusion.2), channel_id=1, source_target_pairs={{0,8},{1,9},{2,10},{3,11},{4,12},{5,13},{6,14},{7,15},{8,0},{9,1},... | collective-permute-start | bytes 417800 | tf_op jit(solution)/shard_map/ppermute | solution.py:65
  714.2 24.2 %collective-permute-start.72 = (bf16[272,640]{1,0:T(8,128)(2,1)S(1)}, bf16[272,640]{1,0:T(8,128)(2,1)S(1)}, u32[]{:S(2)}, u32[]{:S(2)}) collective-permute-start(bf16[272,640]{1,0:T(8,128)(2,1)S(1)} %dynamic-slice_convert_fusion.13), channel_id=1, source_target_pairs={{0,4},{1,5},{2,6},{3,7},{4,0},{5,1},{6,2},{7,3},{8,12},{9,13},{10,... | collective-permute-start | bytes 1044488 | tf_op jit(solution)/shard_map/ppermute | solution.py:65
  718.2 28.6 %collective-permute-start.67 = (bf16[272,512]{1,0:T(8,128)(2,1)S(1)}, bf16[272,512]{1,0:T(8,128)(2,1)S(1)}, u32[]{:S(2)}, u32[]{:S(2)}) collective-permute-start(bf16[272,512]{1,0:T(8,128)(2,1)S(1)} %maximum_select_fusion.31), channel_id=1, source_target_pairs={{0,4},{1,5},{2,6},{3,7},{4,0},{5,1},{6,2},{7,3},{8,12},{9,13},{10,... | collective-permute-start | bytes 835592 | tf_op jit(solution)/shard_map/ppermute | solution.py:65
  718.3 16.6 %collective-permute-start.49 = (bf16[40,2048]{1,0:T(8,128)(2,1)S(1)}, bf16[40,2048]{1,0:T(8,128)(2,1)S(1)}, u32[]{:S(2)}, u32[]{:S(2)}) collective-permute-start(bf16[40,2048]{1,0:T(8,128)(2,1)S(1)} %fusion.61), channel_id=1, source_target_pairs={{0,8},{1,9},{2,10},{3,11},{4,12},{5,13},{6,14},{7,15},{8,0},{9,1},... | collective-permute-start | bytes 491528 | tf_op jit(solution)/shard_map/ppermute | solution.py:65
  735.0 11.1 %collective-permute-start.56 = (bf16[40,2256]{1,0:T(8,128)(2,1)S(1)}, bf16[40,2256]{1,0:T(8,128)(2,1)S(1)}, u32[]{:S(2)}, u32[]{:S(2)}) collective-permute-start(bf16[40,2256]{1,0:T(8,128)(2,1)S(1)} %fusion.58), channel_id=1, source_target_pairs={{0,8},{1,9},{2,10},{3,11},{4,12},{5,13},{6,14},{7,15},{8,0},{9,1},... | collective-permute-start | bytes 541448 | tf_op jit(solution)/shard_map/ppermute | solution.py:65
  738.4 24.4 %collective-permute-start.50 = (bf16[72,2048]{1,0:T(8,128)(2,1)S(1)}, bf16[72,2048]{1,0:T(8,128)(2,1)S(1)}, u32[]{:S(2)}, u32[]{:S(2)}) collective-permute-start(bf16[72,2048]{1,0:T(8,128)(2,1)S(1)} %fusion.63), channel_id=1, source_target_pairs={{0,4},{1,5},{2,6},{3,7},{4,0},{5,1},{6,2},{7,3},{8,12},{9,13},{10,... | collective-permute-start | bytes 884744 | tf_op jit(solution)/shard_map/ppermute | solution.py:65
  746.8 9.7 %collective-permute-start.57 = (bf16[40,2256]{1,0:T(8,128)(2,1)S(1)}, bf16[40,2256]{1,0:T(8,128)(2,1)S(1)}, u32[]{:S(2)}, u32[]{:S(2)}) collective-permute-start(bf16[40,2256]{1,0:T(8,128)(2,1)S(1)} %fusion.57), channel_id=1, source_target_pairs={{0,8},{1,9},{2,10},{3,11},{4,12},{5,13},{6,14},{7,15},{8,0},{9,1},... | collective-permute-start | bytes 541448 | tf_op jit(solution)/shard_map/ppermute | solution.py:65
  752.8 15.0 %collective-permute-start.68 = (bf16[544,512]{1,0:T(8,128)(2,1)S(1)}, bf16[544,512]{1,0:T(8,128)(2,1)S(1)}, u32[]{:S(2)}, u32[]{:S(2)}) collective-permute-start(bf16[544,512]{1,0:T(8,128)(2,1)S(1)} %maximum_select_fusion.23), channel_id=1, source_target_pairs={{0,2},{1,3},{2,0},{3,1},{4,6},{5,7},{6,4},{7,5},{8,10},{9,11},{10,... | collective-permute-start | bytes 1671176 | tf_op jit(solution)/shard_map/ppermute | solution.py:65
  759.1 8.6 %collective-permute-start.58 = (bf16[72,2256]{1,0:T(8,128)(2,1)S(1)}, bf16[72,2256]{1,0:T(8,128)(2,1)S(1)}, u32[]{:S(2)}, u32[]{:S(2)}) collective-permute-start(bf16[72,2256]{1,0:T(8,128)(2,1)S(1)} %fusion.59), channel_id=1, source_target_pairs={{0,4},{1,5},{2,6},{3,7},{4,0},{5,1},{6,2},{7,3},{8,12},{9,13},{10,... | collective-permute-start | bytes 974600 | tf_op jit(solution)/shard_map/ppermute | solution.py:65
  763.0 16.9 %collective-permute-start.51 = (bf16[144,2048]{1,0:T(8,128)(2,1)S(1)}, bf16[144,2048]{1,0:T(8,128)(2,1)S(1)}, u32[]{:S(2)}, u32[]{:S(2)}) collective-permute-start(bf16[144,2048]{1,0:T(8,128)(2,1)S(1)} %maximum_select_fusion.22), channel_id=1, source_target_pairs={{0,2},{1,3},{2,0},{3,1},{4,6},{5,7},{6,4},{7,5},{8,10},{9,11},{10,... | collective-permute-start | bytes 1769480 | tf_op jit(solution)/shard_map/ppermute | solution.py:65
  763.1 9.0 %collective-permute-start.75 = (bf16[272,640]{1,0:T(8,128)(2,1)S(1)}, bf16[272,640]{1,0:T(8,128)(2,1)S(1)}, u32[]{:S(2)}, u32[]{:S(2)}) collective-permute-start(bf16[272,640]{1,0:T(8,128)(2,1)S(1)} %maximum_select_fusion.29), channel_id=1, source_target_pairs={{0,4},{1,5},{2,6},{3,7},{4,0},{5,1},{6,2},{7,3},{8,12},{9,13},{10,... | collective-permute-start | bytes 1044488 | tf_op jit(solution)/shard_map/ppermute | solution.py:65
  767.8 17.8 %collective-permute-start.59 = (bf16[144,2256]{1,0:T(8,128)(2,1)S(1)}, bf16[144,2256]{1,0:T(8,128)(2,1)S(1)}, u32[]{:S(2)}, u32[]{:S(2)}) collective-permute-start(bf16[144,2256]{1,0:T(8,128)(2,1)S(1)} %maximum_select_fusion.20), channel_id=1, source_target_pairs={{0,1},{1,0},{2,3},{3,2},{4,5},{5,4},{6,7},{7,6},{8,9},{9,8},{10,11... | collective-permute-start | bytes 1949192 | tf_op jit(solution)/shard_map/ppermute | solution.py:65
  768.4 49.6 %collective-permute-start.69 = (bf16[1080,512]{1,0:T(8,128)(2,1)S(1)}, bf16[1080,512]{1,0:T(8,128)(2,1)S(1)}, u32[]{:S(2)}, u32[]{:S(2)}) collective-permute-start(bf16[1080,512]{1,0:T(8,128)(2,1)S(1)} %fusion.55), channel_id=1, source_target_pairs={{0,1},{1,0},{2,3},{3,2},{4,5},{5,4},{6,7},{7,6},{8,9},{9,8},{10,11... | collective-permute-start | bytes 3317768 | tf_op jit(solution)/shard_map/ppermute | solution.py:65
  772.4 44.8 %collective-permute-start.76 = (bf16[544,640]{1,0:T(8,128)(2,1)S(1)}, bf16[544,640]{1,0:T(8,128)(2,1)S(1)}, u32[]{:S(2)}, u32[]{:S(2)}) collective-permute-start(bf16[544,640]{1,0:T(8,128)(2,1)S(1)} %maximum_select_fusion.19), channel_id=1, source_target_pairs={{0,1},{1,0},{2,3},{3,2},{4,5},{5,4},{6,7},{7,6},{8,9},{9,8},{10,11... | collective-permute-start | bytes 2088968 | tf_op jit(solution)/shard_map/ppermute | solution.py:65
  780.3 49.5 %collective-permute-start.52 = (bf16[288,2048]{1,0:T(8,128)(2,1)S(1)}, bf16[288,2048]{1,0:T(8,128)(2,1)S(1)}, u32[]{:S(2)}, u32[]{:S(2)}) collective-permute-start(bf16[288,2048]{1,0:T(8,128)(2,1)S(1)} %maximum_select_fusion.15), channel_id=1, source_target_pairs={{0,1},{1,0},{2,3},{3,2},{4,5},{5,4},{6,7},{7,6},{8,9},{9,8},{10,11... | collective-permute-start | bytes 3538952 | tf_op jit(solution)/shard_map/ppermute | solution.py:65
  786.0 45.0 %collective-permute-start.60 = (bf16[288,2256]{1,0:T(8,128)(2,1)S(1)}, bf16[288,2256]{1,0:T(8,128)(2,1)S(1)}, u32[]{:S(2)}, u32[]{:S(2)}) collective-permute-start(bf16[288,2256]{1,0:T(8,128)(2,1)S(1)} %maximum_select_fusion.14), channel_id=1, source_target_pairs={{0,2},{1,3},{2,0},{3,1},{4,6},{5,7},{6,4},{7,5},{8,10},{9,11},{10,... | collective-permute-start | bytes 3898376 | tf_op jit(solution)/shard_map/ppermute | solution.py:65
  817.7 19.3 %collective-permute-start.77 = (bf16[1080,640]{1,0:T(8,128)(2,1)S(1)}, bf16[1080,640]{1,0:T(8,128)(2,1)S(1)}, u32[]{:S(2)}, u32[]{:S(2)}) collective-permute-start(bf16[1080,640]{1,0:T(8,128)(2,1)S(1)} %fusion.50), channel_id=1, source_target_pairs={{0,2},{1,3},{2,0},{3,1},{4,6},{5,7},{6,4},{7,5},{8,10},{9,11},{10,... | collective-permute-start | bytes 4147208 | tf_op jit(solution)/shard_map/ppermute | solution.py:65
  (71 other events, 812.8 us)
